TPU v7x, 128 devices: a whole 4x4x4 slice. The times are simulated.
128 devices in a mesh: section: 4 (over z_hi, core), lane: 32 (over x, y, z_lo).
Axes of the slice: x: 4, y: 4, z: 4 (z_hi: 2, z_lo: 2; z = z_hi * 2 + z_lo), core: 2. Of those that a mesh axis runs over, the one named last changes fastest.
Arguments:
- voltages: bfloat16 [2, 2048, 49152], P(None, ('section', 'lane')), may hold values from -6 to 6
- earlier_covariance: bfloat16 [128, 2, 2048, 2048], P(('section', 'lane')), may hold values from -0.25 to 16, as said below
- antenna_pos: int32 [2048], replicated, may hold values from 0 to 4095
- beam_dir: int32 [128], replicated, may hold values from 0 to 4095
Outputs:
- timeseries: float32 [128, 2, 49152], P(('section', 'lane'))
Inputs may be any that keep to these rules, and one draw needn't show every extreme that they name: `earlier_covariance`: each channel's matrix is Hermitian: part 0 symmetric, part 1 antisymmetric with zero diagonal, and positive definite.
All inputs are finite; a program needn't handle non-finite values.
Results may differ from a plain program's by a relative error of at most 0.0075.
Values may be sent and summed in bfloat16 or wider, within the bound.
No kernel may reach another device: no remote copies, remote signals or barrier semaphores. Data moves between devices by JAX's collectives and lax.ppermute only.
A program may use at most 192 MiB of HBM per device.

v0:
```python
import math

import jax
import jax.numpy as jnp
from jax import lax
from jax.sharding import PartitionSpec as P

FREQUENCY_BINS = 128
CHEB = 2
LOAD_PCT = 10
KEEP_PCT = 50


phase_steps = 4096


def shortened(value):
    return jax.tree.map(lambda a: a.astype(jnp.bfloat16) if a.dtype == jnp.float32 else a, value)


def padded_2(cells, sides, width):
    for axis, dim in sides:
        count = lax.axis_size(axis)
        ends = count - 1
        head = lax.slice_in_dim(cells, 0, width, axis=dim)
        tail = lax.slice_in_dim(cells, cells.shape[dim] - width, cells.shape[dim], axis=dim)
        cells = jnp.concatenate(
            [
                lax.ppermute(tail, axis, [(i, (i + 1) % count) for i in range(ends)]),
                cells,
                lax.ppermute(head, axis, [((i + 1) % count, i) for i in range(ends)]),
            ],
            axis=dim,
        )
    return cells


def fourier_matrix(length, sign):
    counter = jnp.arange(length, dtype=jnp.int32)
    angle = (counter[:, None] * counter[None, :] % length).astype(jnp.float32) * (
        2.0 * math.pi / length
    )
    cosine = jnp.cos(angle) / math.sqrt(length)
    sine = sign * jnp.sin(angle) / math.sqrt(length)
    return jnp.stack(
        [jnp.stack([cosine, sine], axis=1), jnp.stack([-sine, cosine], axis=1)], axis=0
    ).astype(jnp.bfloat16)


def apply_matrix(cov_real, cov_imag, loading, vector):
    half = vector.shape[1] // 2
    high = lax.Precision.HIGHEST
    with_real = jnp.dot(cov_real, vector, precision=high, preferred_element_type=jnp.float32)
    with_imag = jnp.dot(cov_imag, vector, precision=high, preferred_element_type=jnp.float32)
    out_real = with_real[:, :half] - with_imag[:, half:] + loading * vector[:, :half]
    out_imag = with_imag[:, :half] + with_real[:, half:] + loading * vector[:, half:]
    return jnp.concatenate([out_real, out_imag], axis=1)


def compute_beam_weights(spectrum, prior, channel, antenna_pos, beam_dir):
    voltage_samples = spectrum.shape[-1]
    antennas = spectrum.shape[1]
    stacked = jnp.concatenate([spectrum[0], spectrum[1]], axis=1)
    rotated = jnp.concatenate([spectrum[1], -spectrum[0]], axis=1)
    data_real = jnp.dot(stacked, stacked.T, preferred_element_type=jnp.float32)
    data_imag = jnp.dot(rotated, stacked.T, preferred_element_type=jnp.float32)
    keep = KEEP_PCT / 100.0
    cov_real = keep * prior[0].astype(jnp.float32) + (1.0 - keep) / voltage_samples * data_real
    cov_imag = keep * prior[1].astype(jnp.float32) + (1.0 - keep) / voltage_samples * data_imag
    mean_diag = jnp.trace(cov_real) / antennas
    loading = LOAD_PCT / 100.0 * mean_diag
    upper = 5.0 * mean_diag
    phase_int = (
        antenna_pos[:, None]
        * beam_dir[None, :]
        % phase_steps
        * (channel + FREQUENCY_BINS)
        % phase_steps
    )
    angle = phase_int.astype(jnp.float32) * (2.0 * math.pi / phase_steps)
    remain = jnp.concatenate([jnp.cos(angle), jnp.sin(angle)], axis=1)
    center = 0.5 * (upper + loading)
    radius = 0.5 * (upper - loading)
    ratio = center / radius
    factor = 1.0 / ratio
    iterate = jnp.zeros_like(remain)
    update = remain / center
    for step in range(CHEB):
        iterate = iterate + update
        if step + 1 < CHEB:
            remain = remain - apply_matrix(cov_real, cov_imag, loading, update)
            factor_next = 1.0 / (2.0 * ratio - factor)
            update = factor_next * factor * update + 2.0 * factor_next / radius * remain
            factor = factor_next
    half = iterate.shape[1] // 2
    return jnp.stack([iterate[:, :half], iterate[:, half:]], axis=0).astype(jnp.bfloat16)


def project(beam_weight_set, spectra):
    rotated = jnp.stack([spectra, jnp.stack([spectra[:, 1], -spectra[:, 0]], axis=1)], axis=1)
    return jnp.einsum(
        "npab,nqpas->nqbs", beam_weight_set, rotated, preferred_element_type=jnp.float32
    )


def shards(voltages, earlier_covariance, antenna_pos, beam_dir):
    chans = earlier_covariance.shape[0]
    antenna_coordinates = voltages.shape[1]
    voltage_samples = voltages.shape[2] // FREQUENCY_BINS
    tapered_signal = voltages.reshape(2, antenna_coordinates, voltage_samples, FREQUENCY_BINS)
    spectra = jnp.einsum(
        "past,ptqk->kqas",
        tapered_signal,
        fourier_matrix(FREQUENCY_BINS, -1.0),
        preferred_element_type=jnp.float32,
    ).astype(jnp.bfloat16)
    spectra_here = lax.all_to_all(
        spectra, ("section", "lane"), split_axis=0, concat_axis=2, tiled=True
    )
    first_channel = lax.axis_index(("section", "lane")) * chans
    channel_ids = first_channel + jnp.arange(chans, dtype=jnp.int32)

    def solve_item(item):
        return compute_beam_weights(item[0], item[1], item[2], antenna_pos, beam_dir)

    beam_weight_set = lax.map(solve_item, (spectra_here, earlier_covariance, channel_ids))
    padded = padded_2(shortened(beam_weight_set), ((("section", "lane"), 0),), 1).astype(
        beam_weight_set.dtype
    )
    total = (
        project(padded[:-2], spectra_here)
        + 2.0 * project(padded[1:-1], spectra_here)
        + project(padded[2:], spectra_here)
    )
    beamed = (0.25 * total).astype(jnp.bfloat16)
    turned = lax.all_to_all(beamed, ("section", "lane"), split_axis=2, concat_axis=0, tiled=True)
    beam_loc = turned.shape[2]
    series = jnp.einsum(
        "kpbs,pkqt->bqst",
        turned,
        fourier_matrix(FREQUENCY_BINS, 1.0),
        preferred_element_type=jnp.float32,
    )
    return series.reshape(beam_loc, 2, voltage_samples * FREQUENCY_BINS)


def solution(mesh):
    placed = (
        P(None, ("section", "lane"), None),
        P(("section", "lane"), None, None, None),
        P(),
        P(),
    )
    return jax.shard_map(
        shards,
        mesh=mesh,
        in_specs=placed,
        out_specs=P(("section", "lane"), None, None),
        check_vma=False,
    )
```

profile of v0, /device:TPU:1, one launch (start us, length us, event | category | flops | bytes accessed | tf_op | source)
XLA Modules:
  0.0 211.3 jit_solution(17853474496370549034)
XLA Ops:
  0.0 0.3 negate_convert_fusion
  0.3 0.3 multiply_convert_fusion
  0.6 0.3 multiply_convert_fusion.2
  0.8 2.6 %copy.56 = bf16[4,8,384,128]{3,2,1,0:T(8,128)(2,1)S(1)} copy(bf16[4,8,384,128]{3,1,2,0:T(8,128)(2,1)} %bitcast.151) | data formatting | bytes 6291456
  3.5 1.0 fusion.11
  4.5 3.5 %copy.30 = bf16[128,2,16,384]{3,2,1,0:T(8,128)(2,1)} copy(bf16[128,2,16,384]{3,0,2,1:T(8,128)(2,1)S(1)} %fusion.11) | data formatting | bytes 6291456 | tf_op jit(solution)/shard_map/convert_element_type | solution.py:116
  8.1 11.9 %all-to-all-start = ((bf16[128,2,16,384]{3,2,1,0:T(8,128)(2,1)}), bf16[128,2,16,384]{3,2,1,0:T(8,128)(2,1)}, u32[]{:S(2)}, u32[]{:S(2)}) async-start(bf16[128,2,16,384]{3,2,1,0:T(8,128)(2,1)} %copy.30), calls=%async_computation | async-start | bytes 6291456 | tf_op jit(solution)/shard_map/all_to_all | solution.py:117
  20.0 0.0 copy-done.10
  20.0 0.0 copy-done.11
  20.0 6.1 %fusion.50 = (f32[2048,128]{0,1:T(8,128)}, f32[2048,128]{0,1:T(8,128)}) fusion(s32[]{:T(128)S(6)} %add.114, s32[128]{0:T(128)S(1)} %copy-done.11, s32[2048]{0:T(1024)S(1)} %copy-done.10), kind=kLoop, calls=%fused_computation.75 | loop fusion | flops 6815744 | bytes 2105860 | tf_op jit(solution)/shard_map/while/body/eval_jaxpr/cos | solution.py:81
  26.1 34.9 %all-to-all-done = bf16[128,2,16,384]{3,2,1,0:T(8,128)(2,1)} async-done(((bf16[128,2,16,384]{3,2,1,0:T(8,128)(2,1)}), bf16[128,2,16,384]{3,2,1,0:T(8,128)(2,1)}, u32[]{:S(2)}, u32[]{:S(2)}) %all-to-all-start) | async-done | bytes 3145760 | tf_op jit(solution)/shard_map/all_to_all | solution.py:117
  61.0 2.2 %copy.69 = bf16[128,2,16,384]{3,2,0,1:T(8,128)(2,1)S(1)} copy(bf16[128,2,16,384]{3,2,1,0:T(8,128)(2,1)} %all-to-all-done) | data formatting | bytes 6291456 | tf_op jit(solution)/shard_map/all_to_all | solution.py:117
  63.2 0.3 fusion.86
  63.5 0.0 copy-start.2
  63.5 0.0 copy-start.6
  63.5 14.8 %select_reduce_fusion = (f32[]{:T(128)}, f32[2048,2048]{1,0:T(8,128)}) fusion(bf16[1,2,2048,2048]{3,2,1,0:T(8,128)(2,1)} %param.5, bf16[2048,384]{1,0:T(8,128)(2,1)S(1)} %bitcast.153, bf16[2048,384]{1,0:T(8,128)(2,1)S(1)} %bitcast.149), kind=kOutput, calls=%fused_computation.6 | convolution fusion | flops 6478102528 | bytes 28311556 | tf_op jit(solution)/shard_map/while/body/eval_jaxpr/dot_general | solution.py:65
  78.3 0.0 copy-done.6
  79.8 2.7 %bitcast_negate_fusion = bf16[2048,384]{1,0:T(8,128)(2,1)} fusion(bf16[1,1,128,16,384]{4,3,2,1,0:T(8,128)(2,1)} %copy-done.2), kind=kLoop, calls=%fused_computation.118 | loop fusion | flops 786432 | bytes 3145728 | tf_op jit(solution)/shard_map/while/body/eval_jaxpr/neg | solution.py:64
  82.5 2.0 fusion.28
  84.5 0.2 copy-done.1
  84.7 20.5 %fusion.4 = f32[2048,256]{0,1:T(8,128)S(1)} fusion(f32[2048,2048]{1,0:T(8,128)} %get-tuple-element.45, bf16[1,2,2048,2048]{3,2,1,0:T(8,128)(2,1)} %param.5, f32[2048,128]{0,1:T(8,128)S(1)} %copy-done.1, f32[2048,128]{0,1:T(8,128)S(1)} %copy-done, f32[]{:T(128)S(6)} %mul.275), kind=kOutput, calls=%fused_computation.8 | convolution fusion | flops 12902727680 | bytes 29360132 | tf_op jit(solution)/shard_map/while/body/eval_jaxpr/dot_general | solution.py:53
  105.3 9.6 %fusion.12 = f32[2048,2048]{1,0:T(8,128)} fusion(bf16[2048,384]{1,0:T(8,128)(2,1)S(1)} %copy-done.5, bf16[2048,384]{1,0:T(8,128)(2,1)S(1)} %bitcast.154, bf16[2048,384]{1,0:T(8,128)(2,1)S(1)} %bitcast.150), kind=kOutput, calls=%fused_computation.20 | convolution fusion | flops 6455033856 | bytes 21495808 | tf_op jit(solution)/shard_map/while/body/eval_jaxpr/dot_general | solution.py:66
  114.9 20.4 %fusion = f32[2048,256]{0,1:T(8,128)S(1)} fusion(f32[2048,2048]{1,0:T(8,128)} %fusion.12, bf16[1,2,2048,2048]{3,2,1,0:T(8,128)(2,1)} %param.5, f32[2048,128]{0,1:T(8,128)S(1)} %copy-done.1, f32[2048,128]{0,1:T(8,128)S(1)} %copy-done, f32[]{:T(128)S(6)} %mul.275), kind=kOutput, calls=%fused_computation.1 | convolution fusion | flops 12902727680 | bytes 29360132 | tf_op jit(solution)/shard_map/while/body/eval_jaxpr/dot_general | solution.py:54
  135.3 0.7 fusion.44
  136.0 0.5 fusion.23
  136.5 1.2 fusion.51
  137.7 1.1 pad_maximum_fusion.4
  138.7 4.1 %collective-permute-start.1 = (bf16[1,2,2048,128]{2,3,1,0:T(8,128)(2,1)}, bf16[1,2,2048,128]{2,3,1,0:T(8,128)(2,1)}, u32[]{:S(2)}, u32[]{:S(2)}) collective-permute-start(bf16[1,2,2048,128]{2,3,1,0:T(8,128)(2,1)} %pad_maximum_fusion.4), channel_id=1, source_target_pairs={{1,0},{2,1},{3,2},{4,3},{5,4},{6,5},{7,6},{8,7},{9,8},{10,9},{11,1... | collective-permute-start | bytes 3145736 | tf_op jit(solution)/shard_map/ppermute | solution.py:31
  142.9 1.9 collective-permute-start
  144.8 2.0 fusion.87
  146.8 2.6 %copy.55 = bf16[1,1,2048,384]{2,3,1,0:T(8,128)(2,1)} copy(bf16[1,1,2048,384]{3,2,1,0:T(8,128)(2,1)} %get-tuple-element.33) | data formatting | bytes 3145728
  149.4 3.0 %neg.34 = bf16[1,1,2048,384]{2,3,1,0:T(8,128)(2,1)} negate(bf16[1,1,2048,384]{2,3,1,0:T(8,128)(2,1)} %copy.55) | non-fusion elementwise | flops 786432 | bytes 3145728 | tf_op jit(solution)/shard_map/neg | solution.py:100
  152.4 2.6 %copy.54 = bf16[1,1,2048,384]{2,3,1,0:T(8,128)(2,1)} copy(bf16[1,1,2048,384]{3,2,1,0:T(8,128)(2,1)} %get-tuple-element.32) | data formatting | bytes 3145728
  155.0 2.9 %copy.34 = bf16[1,1,2,2048,384]{3,4,2,1,0:T(8,128)(2,1)} copy(bf16[1,1,2,2048,384]{4,3,2,1,0:T(8,128)(2,1)S(1)} %bitcast.147) | data formatting | bytes 6291456 | tf_op jit(solution)/shard_map/stack | solution.py:100
  158.0 2.3 %maximum_bitcast_fusion.1 = bf16[1,1,2,2048,384]{3,4,2,1,0:T(8,128)(2,1)S(1)} fusion(bf16[1,1,2048,384]{2,3,1,0:T(8,128)(2,1)} %neg.34, bf16[1,1,2048,384]{2,3,1,0:T(8,128)(2,1)} %copy.54), kind=kLoop, calls=%fused_computation.18 | loop fusion | flops 1572864 | bytes 6291456 | tf_op jit(solution)/shard_map/stack | solution.py:100
  160.3 0.5 copy-done.4
  160.8 0.1 copy-done.8
  160.9 0.2 copy-done.9
  161.0 1.8 fusion.32
  162.8 12.8 %collective-permute-done.1 = bf16[1,2,2048,128]{2,3,1,0:T(8,128)(2,1)} collective-permute-done((bf16[1,2,2048,128]{2,3,1,0:T(8,128)(2,1)}, bf16[1,2,2048,128]{2,3,1,0:T(8,128)(2,1)}, u32[]{:S(2)}, u32[]{:S(2)}) %collective-permute-start.1) | collective-permute-done | bytes 1048608 | tf_op jit(solution)/shard_map/ppermute | solution.py:31
  175.6 3.0 %fusion.31 = f32[2,384,128]{2,1,0:T(8,128)S(1)} fusion(bf16[1,1,2,2048,384]{3,4,2,1,0:T(8,128)(2,1)S(1)} %maximum_bitcast_fusion.1, bf16[1,1,2,2048,384]{3,4,2,1,0:T(8,128)(2,1)S(1)} %copy-done.4, bf16[1,2,2048,128]{2,3,1,0:T(8,128)(2,1)} %collective-permute-done.1), kind=kOutput, calls=%fused_computation.47 | convolution fusion | flops 808452096 | bytes 7733248 | tf_op jit(solution)/shard_map/npab,nqpas->nqbs/dot_general | solution.py:101
  178.6 9.1 %collective-permute-done = bf16[1,2,2048,128]{2,3,1,0:T(8,128)(2,1)} collective-permute-done((bf16[1,2,2048,128]{2,3,1,0:T(8,128)(2,1)}, bf16[1,2,2048,128]{2,3,1,0:T(8,128)(2,1)}, u32[]{:S(2)}, u32[]{:S(2)}) %collective-permute-start) | collective-permute-done | bytes 1048608 | tf_op jit(solution)/shard_map/ppermute | solution.py:29
  187.7 3.0 %fusion.37 = bf16[1,2,128,384]{2,3,1,0:T(8,128)(2,1)S(1)} fusion(f32[2,384,128]{2,1,0:T(8,128)S(1)} %fusion.31, f32[2,384,128]{2,1,0:T(8,128)S(1)} %fusion.32, bf16[1,1,2,2048,384]{3,4,2,1,0:T(8,128)(2,1)S(1)} %maximum_bitcast_fusion.1, bf16[1,1,2,2048,384]{3,4,2,1,0:T(8,128)(2,1)S(1)} %copy-done.4, bf16[1,2,2048,128]{2,3,1,0:T(8,128)(2,1)} %collective-permute-done), kind=kOutput, calls=%fused_computation.54 | convolution fusion | flops 808845312 | bytes 8323072 | tf_op jit(solution)/shard_map/npab,nqpas->nqbs/dot_general | solution.py:101
  190.8 0.2 copy.38
  191.0 18.9 %all_to_all.33 = bf16[1,2,128,384]{3,1,0,2:T(2,128)(2,1)S(1)} all-to-all(bf16[1,2,128,384]{3,1,0,2:T(2,128)(2,1)S(1)} %copy.38), channel_id=1, replica_groups=mesh['section'=4,'lane'=32] {'section','lane'}, dimensions={2} | all-to-all | bytes 393216 | tf_op jit(solution)/shard_map/all_to_all | solution.py:136
  209.9 0.2 convolution_bitcast_fusion
  210.1 0.2 copy.40
  210.3 1.1 copy.41
  (16 shorter events, 0.0 us)
Async XLA Ops:
  8.1 11.9 %copy-start.10 = (s32[2048]{0:T(1024)S(1)}, s32[2048]{0:T(1024)}, u32[]{:S(2)}) copy-start(s32[2048]{0:T(1024)} %param.6) | copy-start | bytes 24580
  8.1 11.9 %copy-start.11 = (s32[128]{0:T(128)S(1)}, s32[128]{0:T(128)}, u32[]{:S(2)}) copy-start(s32[128]{0:T(128)} %param.7) | copy-start | bytes 1540
  8.1 52.9 %all-to-all-start = ((bf16[128,2,16,384]{3,2,1,0:T(8,128)(2,1)}), bf16[128,2,16,384]{3,2,1,0:T(8,128)(2,1)}, u32[]{:S(2)}, u32[]{:S(2)}) async-start(bf16[128,2,16,384]{3,2,1,0:T(8,128)(2,1)} %copy.30), calls=%async_computation | async-start | bytes 6291456 | tf_op jit(solution)/shard_map/all_to_all | solution.py:117
  63.5 14.8 %copy-start.2 = (bf16[1,1,128,16,384]{4,3,2,1,0:T(8,128)(2,1)}, bf16[1,1,128,16,384]{4,3,2,1,0:T(8,128)(2,1)S(1)}, u32[]{:S(2)}) copy-start(bf16[1,1,128,16,384]{4,3,2,1,0:T(8,128)(2,1)S(1)} %get-tuple-element.19) | copy-start | bytes 4718596
  63.5 14.8 %copy-start.6 = (bf16[1,1,128,16,384]{4,3,2,1,0:T(8,128)(2,1)}, bf16[1,1,128,16,384]{4,3,2,1,0:T(8,128)(2,1)S(1)}, u32[]{:S(2)}) copy-start(bf16[1,1,128,16,384]{4,3,2,1,0:T(8,128)(2,1)S(1)} %get-tuple-element.20) | copy-start | bytes 4718596
  82.5 2.0 copy-start
  82.5 2.2 %copy-start.1 = (f32[2048,128]{0,1:T(8,128)S(1)}, f32[2048,128]{0,1:T(8,128)}, u32[]{:S(2)}) copy-start(f32[2048,128]{0,1:T(8,128)} %get-tuple-element.43) | copy-start | bytes 3145732
  84.7 20.6 %copy-start.3 = (bf16[1,1,128,16,384]{4,3,2,1,0:T(8,128)(2,1)S(1)}, bf16[1,1,128,16,384]{4,3,2,1,0:T(8,128)(2,1)}, u32[]{:S(2)}) copy-start(bf16[1,1,128,16,384]{4,3,2,1,0:T(8,128)(2,1)} %copy-done.2) | copy-start | bytes 4718596
  84.7 20.6 %copy-start.5 = (bf16[2048,384]{1,0:T(8,128)(2,1)S(1)}, bf16[2048,384]{1,0:T(8,128)(2,1)}, u32[]{:S(2)}) copy-start(bf16[2048,384]{1,0:T(8,128)(2,1)} %bitcast_negate_fusion) | copy-start | bytes 4718596
  84.7 20.6 %copy-start.7 = (bf16[1,1,128,16,384]{4,3,2,1,0:T(8,128)(2,1)S(1)}, bf16[1,1,128,16,384]{4,3,2,1,0:T(8,128)(2,1)}, u32[]{:S(2)}) copy-start(bf16[1,1,128,16,384]{4,3,2,1,0:T(8,128)(2,1)} %copy-done.6) | copy-start | bytes 4718596
  138.7 36.9 %collective-permute-start.1 = (bf16[1,2,2048,128]{2,3,1,0:T(8,128)(2,1)}, bf16[1,2,2048,128]{2,3,1,0:T(8,128)(2,1)}, u32[]{:S(2)}, u32[]{:S(2)}) collective-permute-start(bf16[1,2,2048,128]{2,3,1,0:T(8,128)(2,1)} %pad_maximum_fusion.4), channel_id=1, source_target_pairs={{1,0},{2,1},{3,2},{4,3},{5,4},{6,5},{7,6},{8,7},{9,8},{10,9},{11,1... | collective-permute-start | bytes 3145736 | tf_op jit(solution)/shard_map/ppermute | solution.py:31
  142.9 44.8 %collective-permute-start = (bf16[1,2,2048,128]{2,3,1,0:T(8,128)(2,1)}, bf16[1,2,2048,128]{2,3,1,0:T(8,128)(2,1)}, u32[]{:S(2)}, u32[]{:S(2)}) collective-permute-start(bf16[1,2,2048,128]{2,3,1,0:T(8,128)(2,1)} %pad_maximum_fusion.4), channel_id=1, source_target_pairs={{0,1},{1,2},{2,3},{3,4},{4,5},{5,6},{6,7},{7,8},{8,9},{9,10},{10,1... | collective-permute-start | bytes 3145736 | tf_op jit(solution)/shard_map/ppermute | solution.py:29
  157.9 2.8 %copy-start.4 = (bf16[1,1,2,2048,384]{3,4,2,1,0:T(8,128)(2,1)S(1)}, bf16[1,1,2,2048,384]{3,4,2,1,0:T(8,128)(2,1)}, u32[]{:S(2)}) copy-start(bf16[1,1,2,2048,384]{3,4,2,1,0:T(8,128)(2,1)} %copy.34) | copy-start | bytes 9437188
  157.9 2.9 %copy-start.8 = (bf16[1,2048,128]{1,2,0:T(8,128)(2,1)S(1)}, bf16[1,2048,128]{1,2,0:T(8,128)(2,1)}, u32[]{:S(2)}) copy-start(bf16[1,2048,128]{1,2,0:T(8,128)(2,1)} %get-tuple-element.34) | copy-start | bytes 1572868
  157.9 3.1 %copy-start.9 = (bf16[1,2048,128]{1,2,0:T(8,128)(2,1)S(1)}, bf16[1,2048,128]{1,2,0:T(8,128)(2,1)}, u32[]{:S(2)}) copy-start(bf16[1,2048,128]{1,2,0:T(8,128)(2,1)} %get-tuple-element.35) | copy-start | bytes 1572868
where the time goes:
time: 212 us; the launch traced here: 211 us
  matrix products  74.4 us (35%)
  waiting for transfers between devices  56.8 us (27%)
  local copies, waits for them, and re-layouts  22.4 us (11%)
  other arithmetic  19.2 us (9%)
  blocking collectives  18.9 us (9%)
  starting transfers between devices  18 us (8%)
    all_to_all x1, waiting for transfers between devices, shards(): lax.all_to_all(spectra, ('section', 'lane'), split_axis=0, concat_axis=2,...  34.9 us
    dot_general x1, matrix products, apply_matrix(): jnp.dot(cov_real, vector, precision=high, preferred_element_type=jnp.floa...  20.5 us
    dot_general x1, matrix products, apply_matrix(): jnp.dot(cov_imag, vector, precision=high, preferred_element_type=jnp.floa...  20.4 us
    all_to_all x1, blocking collectives, shards(): lax.all_to_all(beamed, ('section', 'lane'), split_axis=2, concat_axis=0,...  18.9 us
    dot_general x1, matrix products, compute_beam_weights(): data_real = jnp.dot(stacked, stacked.T, preferred_element_type=jnp.float32)  14.8 us
    ppermute x1, waiting for transfers between devices, padded_2(): lax.ppermute(head, axis, [((i + 1) % count, i) for i in range(ends)])  12.8 us
    all_to_all x1, starting transfers between devices, shards(): lax.all_to_all(spectra, ('section', 'lane'), split_axis=0, concat_axis=2,...  11.9 us
    dot_general x1, matrix products, compute_beam_weights(): data_imag = jnp.dot(rotated, stacked.T, preferred_element_type=jnp.float32)  9.61 us
  transfers between devices with their start and end apart: 3, of which 3 were waited for; matrix products, arithmetic and copies ran while one was open for 12% of the time, Pallas kernels for 0%

commit v1 on v0

v1 whole, which is shorter than its diff:
```python
import math

import jax
import jax.numpy as jnp
import ml_dtypes
import numpy as np
from jax import lax
from jax.experimental import pallas as pl
from jax.experimental.pallas import tpu as pltpu
from jax.sharding import Mesh
from jax.sharding import PartitionSpec as P

FREQUENCY_BINS = 128
LOAD_PCT = 10
KEEP_PCT = 50
PHASE_STEPS = 4096

PARTS = ("zh", "core", "x", "y", "zl")
SIZES = (2, 2, 4, 4, 2)
SOLVER = ("zh", "zl", "x", "y", "core")
DEVICES = 128

ANTENNAS = 2048
BEAMS = 128
SPECTRA = 384
HERE = 16
CHUNK = 512
COLUMNS = 256

BF = jnp.bfloat16
F32 = jnp.float32
ANY = pl.BlockSpec(memory_space=pl.ANY)
SMEM = pl.BlockSpec(memory_space=pltpu.SMEM)


def solver_index():
    grid = np.arange(DEVICES).reshape(SIZES)
    return np.transpose(grid, (0, 4, 2, 3, 1)).reshape(-1)


def fourier_matrix(length, sign):
    counter = np.arange(length, dtype=np.int64)
    angle = (counter[:, None] * counter[None, :] % length) * (2.0 * math.pi / length)
    cosine = np.cos(angle) / math.sqrt(length)
    sine = sign * np.sin(angle) / math.sqrt(length)
    table = np.stack([np.stack([cosine, sine], axis=1), np.stack([-sine, cosine], axis=1)], axis=0)
    return table.astype(np.float32).astype(ml_dtypes.bfloat16)


def dot(a, b):
    return jnp.dot(a, b, preferred_element_type=F32)


def steering(pos, directions, channel):
    phase = ((pos * directions) & (PHASE_STEPS - 1)) * (channel + FREQUENCY_BINS)
    moved = (phase & (PHASE_STEPS - 1)) + 512
    quadrant = moved >> 10
    x = ((moved & 1023) - 512).astype(F32) * (2.0 * math.pi / PHASE_STEPS)
    y = x * x
    sine = 1.0 / 362880.0
    for c in (-1.0 / 5040.0, 1.0 / 120.0, -1.0 / 6.0, 1.0):
        sine = sine * y + c
    sine = sine * x
    cosine = 1.0 / 40320.0
    for c in (-1.0 / 720.0, 1.0 / 24.0, -0.5, 1.0):
        cosine = cosine * y + c
    odd = (quadrant & 1) == 1
    c = jnp.where(odd, sine, cosine)
    s = jnp.where(odd, cosine, sine)
    c = jnp.where(((quadrant + 1) & 2) == 2, -c, c)
    s = jnp.where((quadrant & 2) == 2, -s, s)
    return c, s


def earlier_kernel(channels, pos, directions, earlier, product, trace, steer, coarse, own):
    j = pl.program_id(0)

    @pl.when(j == 0)
    def _():
        trace[...] = jnp.zeros_like(trace)
        for i in range(ANTENNAS // COLUMNS):
            at = slice(i * COLUMNS, (i + 1) * COLUMNS)
            c, s = steering(pos[:, at], directions[...], channels[0])
            own[:BEAMS, at] = c.astype(BF)
            own[BEAMS:, at] = s.astype(BF)

    here = pl.ds(pl.multiple_of(j * COLUMNS, COLUMNS), COLUMNS)
    c, s = steering(pos[:, here], directions[...], channels[1])
    steer[:BEAMS] = c
    steer[BEAMS:] = s
    coarse[:BEAMS] = c.astype(BF)
    coarse[BEAMS:] = s.astype(BF)
    first = dot(own[...], earlier[0, 0])
    second = dot(own[...], earlier[0, 1])
    product[:BEAMS] = (first[:BEAMS] + second[BEAMS:]).astype(BF)
    product[BEAMS:] = (first[BEAMS:] - second[:BEAMS]).astype(BF)
    square = earlier[0, 0, here, :].astype(F32)
    row = lax.broadcasted_iota(jnp.int32, square.shape, 0)
    column = lax.broadcasted_iota(jnp.int32, square.shape, 1)
    kept = jnp.where(row == column, square, 0.0)
    kept = jnp.sum(kept.reshape(COLUMNS // 8, 8, COLUMNS), axis=0)
    trace[...] += kept[:, :128] + kept[:, 128:]


def earlier_product(channels, pos, directions, earlier):
    steps = ANTENNAS // COLUMNS
    wide = pl.BlockSpec((2 * BEAMS, COLUMNS), lambda j: (0, j))
    return pl.pallas_call(
        earlier_kernel,
        grid=(steps,),
        in_specs=[
            SMEM,
            pl.BlockSpec((1, ANTENNAS), lambda j: (0, 0)),
            pl.BlockSpec((BEAMS, 1), lambda j: (0, 0)),
            pl.BlockSpec((1, 2, ANTENNAS, COLUMNS), lambda j: (0, 0, 0, j)),
        ],
        out_specs=[wide, pl.BlockSpec((8, 128), lambda j: (0, 0)), wide, wide],
        out_shape=[
            jax.ShapeDtypeStruct((2 * BEAMS, ANTENNAS), BF),
            jax.ShapeDtypeStruct((8, 128), F32),
            jax.ShapeDtypeStruct((2 * BEAMS, ANTENNAS), F32),
            jax.ShapeDtypeStruct((2 * BEAMS, ANTENNAS), BF),
        ],
        scratch_shapes=[pltpu.VMEM((2 * BEAMS, ANTENNAS), BF)],
        name="earlier_product",
    )(channels, pos, directions, earlier)


def chunk_copies(here, held, sems, chunk):
    zh, core = divmod(chunk, 2)
    out = []
    for zl in range(2):
        for q in range(2):
            out.append(
                pltpu.make_async_copy(
                    here.at[zh, zl, :, :, core, q],
                    held.at[q, chunk, :, :, zl],
                    sems.at[chunk * 4 + zl * 2 + q],
                )
            )
    return out


HELD = pltpu.VMEM((2, 4, 4, 4, 2, HERE, SPECTRA), BF)


def weights_kernel(here, steer, coarse, product, trace, out, held, steer_v, coarse_v, product_v, sems, more):
    extra = [
        pltpu.make_async_copy(coarse, coarse_v, more.at[0]),
        pltpu.make_async_copy(product, product_v, more.at[1]),
        pltpu.make_async_copy(steer, steer_v, more.at[2]),
    ]
    extra[0].start()
    copies = [chunk_copies(here, held, sems, chunk) for chunk in range(4)]
    for group in copies:
        for c in group:
            c.start()
    extra[1].start()
    extra[2].start()
    extra[0].wait()

    first = jnp.zeros((2 * BEAMS, SPECTRA), F32)
    second = jnp.zeros((2 * BEAMS, SPECTRA), F32)
    power = jnp.zeros((8, SPECTRA), F32)
    for chunk in range(4):
        for c in copies[chunk]:
            c.wait()
        at = slice(chunk * CHUNK, (chunk + 1) * CHUNK)
        xr = held[0, chunk].reshape(CHUNK, SPECTRA)
        xi = held[1, chunk].reshape(CHUNK, SPECTRA)
        first += dot(coarse_v[:, at], xr)
        second += dot(coarse_v[:, at], xi)
        for x in (xr, xi):
            x = x.astype(F32).reshape(CHUNK // 8, 8, SPECTRA)
            power += jnp.sum(x * x, axis=0)
    inner = jnp.concatenate(
        [first[:BEAMS] + second[BEAMS:], first[BEAMS:] - second[:BEAMS]], axis=0
    ).astype(BF)

    keep = KEEP_PCT / 100.0
    fresh = (1.0 - keep) / SPECTRA
    total = jnp.sum(power, keepdims=True) * fresh + jnp.sum(trace[...], keepdims=True) * keep
    mean_diag = total * (1.0 / ANTENNAS)
    loading = LOAD_PCT / 100.0 * mean_diag
    upper = 5.0 * mean_diag
    center = 0.5 * (upper + loading)
    radius = 0.5 * (upper - loading)
    ratio = center / radius
    factor = 1.0 / ratio
    factor_next = 1.0 / (2.0 * ratio - factor)
    beta = 2.0 * factor_next / (radius * center)
    alpha = (1.0 + factor_next * factor) / center + 2.0 * factor_next / radius
    by_steer = alpha - beta * loading
    by_product = -keep * beta
    by_data = -fresh * beta

    extra[1].wait()
    extra[2].wait()
    turned = (((1,), (1,)), ((), ()))
    for chunk in range(4):
        at = slice(chunk * CHUNK, (chunk + 1) * CHUNK)
        xr = held[0, chunk].reshape(CHUNK, SPECTRA)
        xi = held[1, chunk].reshape(CHUNK, SPECTRA)
        p = lax.dot_general(inner, xr, turned, preferred_element_type=F32)
        q = lax.dot_general(inner, xi, turned, preferred_element_type=F32)
        for half, data in ((0, p[:BEAMS] - q[BEAMS:]), (1, p[BEAMS:] + q[:BEAMS])):
            rows = slice(half * BEAMS, (half + 1) * BEAMS)
            out[rows, at] = (
                by_steer * steer_v[rows, at]
                + by_product * product_v[rows, at].astype(F32)
                + by_data * data
            ).astype(BF)


def solve(here, steer, coarse, product, trace):
    return pl.pallas_call(
        weights_kernel,
        in_specs=[ANY, ANY, ANY, ANY, pl.BlockSpec(memory_space=pltpu.VMEM)],
        out_specs=pl.BlockSpec(memory_space=pltpu.VMEM),
        out_shape=jax.ShapeDtypeStruct((2 * BEAMS, ANTENNAS), BF),
        scratch_shapes=[
            HELD,
            pltpu.VMEM((2 * BEAMS, ANTENNAS), F32),
            pltpu.VMEM((2 * BEAMS, ANTENNAS), BF),
            pltpu.VMEM((2 * BEAMS, ANTENNAS), BF),
            pltpu.SemaphoreType.DMA((16,)),
            pltpu.SemaphoreType.DMA((3,)),
        ],
        name="weights",
    )(here, steer, coarse, product, trace)


def beams_kernel(here, lower, own, higher, out, held, sides, sems, more):
    copies = [chunk_copies(here, held, sems, chunk) for chunk in range(4)]
    parts = []
    for chunk in range(4):
        at = pl.ds(chunk * CHUNK, CHUNK)
        parts.append(
            [
                pltpu.make_async_copy(w.at[:, at], sides.at[i, :, at], more.at[chunk * 3 + i])
                for i, w in enumerate((lower, own, higher))
            ]
        )
        for c in parts[chunk] + copies[chunk]:
            c.start()
    first = jnp.zeros((2 * BEAMS, SPECTRA), F32)
    second = jnp.zeros((2 * BEAMS, SPECTRA), F32)
    for chunk in range(4):
        for c in parts[chunk] + copies[chunk]:
            c.wait()
        at = slice(chunk * CHUNK, (chunk + 1) * CHUNK)
        smooth = (
            0.25 * (sides[0, :, at].astype(F32) + sides[2, :, at].astype(F32))
            + 0.5 * sides[1, :, at].astype(F32)
        ).astype(BF)
        first += dot(smooth, held[0, chunk].reshape(CHUNK, SPECTRA))
        second += dot(smooth, held[1, chunk].reshape(CHUNK, SPECTRA))
    out[0] = (first[:BEAMS] + second[BEAMS:]).astype(BF)
    out[1] = (second[:BEAMS] - first[BEAMS:]).astype(BF)


def form_beams(here, lower, own, higher):
    return pl.pallas_call(
        beams_kernel,
        in_specs=[ANY, ANY, ANY, ANY],
        out_specs=pl.BlockSpec(memory_space=pltpu.VMEM),
        out_shape=jax.ShapeDtypeStruct((2, BEAMS, SPECTRA), BF),
        scratch_shapes=[
            HELD,
            pltpu.VMEM((3, 2 * BEAMS, ANTENNAS), BF),
            pltpu.SemaphoreType.DMA((16,)),
            pltpu.SemaphoreType.DMA((12,)),
        ],
        name="form_beams",
    )(here, lower, own, higher)


def shards(voltages, earlier, antenna_pos, beam_dir):
    signal = voltages.reshape(2, HERE, SPECTRA, FREQUENCY_BINS)
    spectra = jnp.einsum(
        "ptqk,past->kqas", fourier_matrix(FREQUENCY_BINS, -1.0), signal, preferred_element_type=F32
    ).astype(BF)
    here = lax.all_to_all(spectra, SOLVER, split_axis=0, concat_axis=0, tiled=True)
    here = here.reshape(2, 2, 4, 4, 2, 2, HERE, SPECTRA)

    channels = jnp.stack([lax.axis_index(PARTS), lax.axis_index(SOLVER)]).astype(jnp.int32)
    product, trace, steer, coarse = earlier_product(
        channels, antenna_pos.reshape(1, ANTENNAS), beam_dir.reshape(BEAMS, 1), earlier
    )
    swap = [(0, 0), (1, 2), (2, 1), (3, 3)]
    product = lax.ppermute(product, ("core", "zl"), swap)
    trace = lax.ppermute(trace, ("core", "zl"), swap)

    weights = solve(here, steer, coarse, product, trace)

    holder = np.argsort(solver_index()).tolist()
    lower = lax.ppermute(weights, PARTS, list(zip(holder[:-1], holder[1:])))
    higher = lax.ppermute(weights, PARTS, list(zip(holder[1:], holder[:-1])))
    beamed = form_beams(here, lower, weights, higher).transpose(1, 0, 2)
    turned = lax.all_to_all(beamed, PARTS, split_axis=0, concat_axis=0, tiled=True)
    inverse = fourier_matrix(FREQUENCY_BINS, 1.0).transpose(1, 0, 2, 3)[solver_index()]
    series = jnp.einsum("kps,kpqt->qst", turned, inverse, preferred_element_type=F32)
    return series.reshape(1, 2, SPECTRA * FREQUENCY_BINS)


def solution(mesh):
    fine = Mesh(mesh.devices.reshape(SIZES), PARTS)
    placed = (P(None, PARTS, None), P(PARTS, None, None, None), P(), P())
    return jax.shard_map(
        shards, mesh=fine, in_specs=placed, out_specs=P(PARTS, None, None), check_vma=False
    )
```

time: 212 us -> 125 us (0.59)
  matrix products: 74.4 us -> 1.22 us
  Pallas kernels: 0 us -> 25.3 us
  other arithmetic: 19.2 us -> 0.66 us
  waiting for transfers between devices: 56.8 us -> 39.6 us
  local copies, waits for them, and re-layouts: 22.4 us -> 11.9 us
  starting transfers between devices: 18 us -> 22.8 us
  blocking collectives: 18.9 us -> 22.8 us
    dot_general x9 -> x2, matrix products: 74.4 us -> 1.22 us  [the longest x1 1.02 us: shards(): jnp.einsum('ptqk,past->kqas', fourier_matrix(FREQUENCY_BINS, -1.0), signa...]
    all_to_all x1, waiting for transfers between devices: 34.9 us -> 0.01 us  [shards(): lax.all_to_all(spectra, SOLVER, split_axis=0, concat_axis=0, tiled=True)]
    pallas_call x0 -> x3, Pallas kernels: none -> 25.3 us  [the longest x1 13.7 us: earlier_product(): pl.pallas_call(earlier_kernel, grid=(steps,), in_specs=[SMEM, pl.BlockSpe...]
    ppermute x2 -> x4, waiting for transfers between devices: 21.9 us -> 39.6 us  [the longest x1 27.6 us: shards(): trace = lax.ppermute(trace, ('core', 'zl'), swap)]
    cos x1 -> x0, other arithmetic: 6.13 us -> none  [compute_beam_weights(): remain = jnp.concatenate([jnp.cos(angle), jnp.sin(angle)], axis=1)]
    neg x2 -> x0, other arithmetic: 5.68 us -> none  [the longest x1 2.97 us: project(): -spectra[:, 0]]
    ppermute x2 -> x4, starting transfers between devices: 6.07 us -> 11.3 us  [the longest x1 3.65 us: shards(): product = lax.ppermute(product, ('core', 'zl'), swap)]
    another operation x2 -> x0, local copies, waits for them, and re-layouts: 4.08 us -> none  [the longest x1 2.92 us: project(): jnp.stack([spectra, jnp.stack([spectra[:, 1], -spectra[:, 0]], axis=1)],...]
  transfers between devices with their start and end apart: 3 -> 5, of which waited for: 3 -> 3; matrix products, arithmetic and copies ran while one was open for 12% -> 1% of each run, Pallas kernels for 0% -> 11%
where the time goes in v1:
time: 125 us; the launch traced here: 124 us
  waiting for transfers between devices  39.6 us (32%)
  Pallas kernels  25.3 us (20%)
  starting transfers between devices  22.8 us (18%)
  blocking collectives  22.8 us (18%)
  local copies, waits for them, and re-layouts  11.9 us (10%)
    ppermute x1, waiting for transfers between devices, shards(): trace = lax.ppermute(trace, ('core', 'zl'), swap)  27.6 us
    all_to_all x1, blocking collectives, shards(): lax.all_to_all(beamed, PARTS, split_axis=0, concat_axis=0, tiled=True)  22.8 us
    pallas_call x1, Pallas kernels, earlier_product(): pl.pallas_call(earlier_kernel, grid=(steps,), in_specs=[SMEM, pl.BlockSpe...  13.7 us
    all_to_all x1, starting transfers between devices, shards(): lax.all_to_all(spectra, SOLVER, split_axis=0, concat_axis=0, tiled=True)  11.5 us
    ppermute x1, waiting for transfers between devices, shards(): higher = lax.ppermute(weights, PARTS, list(zip(holder[1:], holder[:-1])))  10.8 us
    pallas_call x1, Pallas kernels, solve(): pl.pallas_call(weights_kernel, in_specs=[ANY, ANY, ANY, ANY, pl.BlockSpec...  7.08 us
    unnamed x15, local copies, waits for them, and re-layouts  5.3 us
    pallas_call x1, Pallas kernels, form_beams(): pl.pallas_call(beams_kernel, in_specs=[ANY, ANY, ANY, ANY], out_specs=pl....  4.49 us
  transfers between devices with their start and end apart: 5, of which 3 were waited for; matrix products, arithmetic and copies ran while one was open for 1% of the time, Pallas kernels for 11%

profile of v1, /device:TPU:1, one launch (start us, length us, event | category | flops | bytes accessed | tf_op | source)
XLA Modules:
  0.0 124.4 jit_solution(12842890091004637273)
XLA Ops:
  0.0 0.0 copy-start.3
  0.0 2.7 %copy.19 = bf16[4,8,384,128]{3,2,1,0:T(8,128)(2,1)S(1)} copy(bf16[4,8,384,128]{3,1,2,0:T(8,128)(2,1)} %bitcast.44) | data formatting | bytes 6291456
  2.7 0.0 copy-done.3
  2.7 1.0 fusion
  3.7 3.5 %copy.12 = bf16[128,2,16,384]{3,2,1,0:T(8,128)(2,1)} copy(bf16[128,2,16,384]{3,0,2,1:T(8,128)(2,1)S(1)} %fusion) | data formatting | bytes 6291456 | tf_op jit(solution)/shard_map/convert_element_type | solution.py:282
  7.2 0.0 copy-start.6
  7.2 11.5 %all-to-all-start = ((bf16[128,2,16,384]{3,2,1,0:T(8,128)(2,1)}), bf16[128,2,16,384]{3,2,1,0:T(8,128)(2,1)S(1)}, u32[]{:S(2)}, u32[]{:S(2)}) async-start(bf16[128,2,16,384]{3,2,1,0:T(8,128)(2,1)} %copy.12), calls=%async_computation | async-start | bytes 6291456 | tf_op jit(solution)/shard_map/all_to_all | solution.py:283
  18.7 0.0 copy-done.6
  18.7 0.7 copy.13.directions
  19.5 0.7 pad_add_fusion.channels
  20.1 13.7 %earlier_product.1 = (bf16[256,2048]{1,0:T(8,128)(2,1)}, f32[8,128]{1,0:T(8,128)}, f32[256,2048]{1,0:T(8,128)}, bf16[256,2048]{1,0:T(8,128)(2,1)}) custom-call(s32[2]{0:T(128)} %pad_add_fusion.channels, s32[1,2048]{1,0:T(1,128)} %bitcast.46, s32[128,1]{1,0:T(8,128)} %copy.13.directions, bf16[1,2,2048,2048]{3,2,1,0:T(8,128)(2,1)} %earlier.1), custom_call_target="tpu_custom_call" | custom-call | tf_op jit(solution)/shard_map/earlier_product/pallas_call | solution.py:108
  33.8 3.7 %collective-permute-start = (bf16[256,2048]{1,0:T(8,128)(2,1)}, bf16[256,2048]{1,0:T(8,128)(2,1)}, u32[]{:S(2)}, u32[]{:S(2)}) collective-permute-start(bf16[256,2048]{1,0:T(8,128)(2,1)} %get-tuple-element.11), channel_id=1, source_target_pairs={{0,0},{1,32},{32,1},{33,33},{2,2},{3,34},{34,3},{35,35},{4,4},{5,3... | collective-permute-start | bytes 3145736 | tf_op jit(solution)/shard_map/ppermute | solution.py:291
  37.5 1.9 %collective-permute-start.1 = (f32[8,128]{1,0:T(8,128)}, f32[8,128]{1,0:T(8,128)S(1)}, u32[]{:S(2)}, u32[]{:S(2)}) collective-permute-start(f32[8,128]{1,0:T(8,128)} %get-tuple-element.12), channel_id=1, source_target_pairs={{0,0},{1,32},{32,1},{33,33},{2,2},{3,34},{34,3},{35,35},{4,4},{5,3... | collective-permute-start | bytes 12296 | tf_op jit(solution)/shard_map/ppermute | solution.py:292
  39.4 27.6 %collective-permute-done.1.trace = f32[8,128]{1,0:T(8,128)S(1)} collective-permute-done((f32[8,128]{1,0:T(8,128)}, f32[8,128]{1,0:T(8,128)S(1)}, u32[]{:S(2)}, u32[]{:S(2)}) %collective-permute-start.1) | collective-permute-done | bytes 4128 | tf_op jit(solution)/shard_map/ppermute | solution.py:292
  67.0 0.0 copy-start.5
  67.0 0.0 collective-permute-done.product
  67.0 0.0 all-to-all-done
  67.0 0.0 copy-start
  67.0 0.6 copy-done.5
  67.6 1.1 copy-done
  68.6 7.1 %weights.1.own = bf16[256,2048]{1,0:T(8,128)(2,1)} custom-call(bf16[2,2,4,4,2,2,16,384]{7,6,5,4,3,2,1,0:T(8,128)(2,1)} %bitcast.41, f32[256,2048]{1,0:T(8,128)} %get-tuple-element.9.steer, bf16[256,2048]{1,0:T(8,128)(2,1)} %get-tuple-element.10.coarse, bf16[256,2048]{1,0:T(8,128)(2,1)} %collective-permute-done.product, f32[8,128]{1,0:T(8,128)} %copy-done.5), custom_call_target="tpu_custom_call" | custom-call | tf_op jit(solution)/shard_map/weights/pallas_call | solution.py:216
  75.7 0.0 copy-start.4
  75.7 2.1 %collective-permute-start.3 = (bf16[256,2048]{1,0:T(8,128)(2,1)}, bf16[256,2048]{1,0:T(8,128)(2,1)S(1)}, u32[]{:S(2)}, u32[]{:S(2)}) collective-permute-start(bf16[256,2048]{1,0:T(8,128)(2,1)} %weights.1.own), channel_id=1, source_target_pairs={{32,0},{2,32},{34,2},{4,34},{36,4},{6,36},{38,6},{8,38},{40,8},{10... | collective-permute-start | bytes 3145736 | tf_op jit(solution)/shard_map/ppermute | solution.py:298
  77.8 3.6 %collective-permute-start.2 = (bf16[256,2048]{1,0:T(8,128)(2,1)}, bf16[256,2048]{1,0:T(8,128)(2,1)S(1)}, u32[]{:S(2)}, u32[]{:S(2)}) collective-permute-start(bf16[256,2048]{1,0:T(8,128)(2,1)} %weights.1.own), channel_id=1, source_target_pairs={{0,32},{32,2},{2,34},{34,4},{4,36},{36,6},{6,38},{38,8},{8,40},{40... | collective-permute-start | bytes 3145736 | tf_op jit(solution)/shard_map/ppermute | solution.py:297
  81.4 10.8 %collective-permute-done.3.higher = bf16[256,2048]{1,0:T(8,128)(2,1)S(1)} collective-permute-done((bf16[256,2048]{1,0:T(8,128)(2,1)}, bf16[256,2048]{1,0:T(8,128)(2,1)S(1)}, u32[]{:S(2)}, u32[]{:S(2)}) %collective-permute-start.3) | collective-permute-done | bytes 1048608 | tf_op jit(solution)/shard_map/ppermute | solution.py:298
  92.2 0.0 copy-start.1
  92.2 1.3 %collective-permute-done.2.lower = bf16[256,2048]{1,0:T(8,128)(2,1)S(1)} collective-permute-done((bf16[256,2048]{1,0:T(8,128)(2,1)}, bf16[256,2048]{1,0:T(8,128)(2,1)S(1)}, u32[]{:S(2)}, u32[]{:S(2)}) %collective-permute-start.2) | collective-permute-done | bytes 1048608 | tf_op jit(solution)/shard_map/ppermute | solution.py:297
  93.5 0.0 copy-done.1
  93.5 0.0 copy-start.2
  93.5 1.0 copy-done.2
  94.5 4.5 %form_beams.1 = bf16[2,128,384]{2,1,0:T(8,128)(2,1)} custom-call(bf16[2,2,4,4,2,2,16,384]{7,6,5,4,3,2,1,0:T(8,128)(2,1)} %bitcast.42, bf16[256,2048]{1,0:T(8,128)(2,1)} %copy-done.2, bf16[256,2048]{1,0:T(8,128)(2,1)} %weights.1.own, bf16[256,2048]{1,0:T(8,128)(2,1)} %copy-done.1), custom_call_target="tpu_custom_call" | custom-call | tf_op jit(solution)/shard_map/form_beams/pallas_call | solution.py:263
  99.0 1.1 copy.14
  100.1 22.8 %all_to_all.10 = bf16[128,2,384]{2,1,0:T(2,128)(2,1)S(1)} all-to-all(bf16[128,2,384]{2,1,0:T(2,128)(2,1)S(1)} %copy.14), channel_id=1, replica_groups=mesh['zh'=2,'core'=2,'x'=4,'y'=4,'zl'=2] {'zh','core','x','y','zl'}, dimensions={0} | all-to-all | bytes 393216 | tf_op jit(solution)/shard_map/all_to_all | solution.py:300
  122.9 0.2 copy.15
  123.2 0.0 copy-done.4
  123.2 0.2 convolution_bitcast_fusion
  123.4 1.0 reshape.19
Async XLA Ops:
  0.0 2.7 %copy-start.3 = (bf16[2,128,2,128,1]{1,3,0,4,2:T(8,128)(2,1)S(1)}, bf16[2,128,2,128,1]{1,3,0,4,2:T(8,128)(2,1)}, u32[]{:S(2)}) copy-start(bf16[2,128,2,128,1]{1,3,0,4,2:T(8,128)(2,1)} %constant.35) | copy-start | bytes 393220
  7.2 11.5 %copy-start.6 = (s32[128]{0:T(128)S(1)}, s32[128]{0:T(128)}, u32[]{:S(2)}) copy-start(s32[128]{0:T(128)} %param.9) | copy-start | bytes 1540
  7.2 59.8 %all-to-all-start = ((bf16[128,2,16,384]{3,2,1,0:T(8,128)(2,1)}), bf16[128,2,16,384]{3,2,1,0:T(8,128)(2,1)S(1)}, u32[]{:S(2)}, u32[]{:S(2)}) async-start(bf16[128,2,16,384]{3,2,1,0:T(8,128)(2,1)} %copy.12), calls=%async_computation | async-start | bytes 6291456 | tf_op jit(solution)/shard_map/all_to_all | solution.py:283
  33.8 33.2 %collective-permute-start = (bf16[256,2048]{1,0:T(8,128)(2,1)}, bf16[256,2048]{1,0:T(8,128)(2,1)}, u32[]{:S(2)}, u32[]{:S(2)}) collective-permute-start(bf16[256,2048]{1,0:T(8,128)(2,1)} %get-tuple-element.11), channel_id=1, source_target_pairs={{0,0},{1,32},{32,1},{33,33},{2,2},{3,34},{34,3},{35,35},{4,4},{5,3... | collective-permute-start | bytes 3145736 | tf_op jit(solution)/shard_map/ppermute | solution.py:291
  37.5 29.5 %collective-permute-start.1 = (f32[8,128]{1,0:T(8,128)}, f32[8,128]{1,0:T(8,128)S(1)}, u32[]{:S(2)}, u32[]{:S(2)}) collective-permute-start(f32[8,128]{1,0:T(8,128)} %get-tuple-element.12), channel_id=1, source_target_pairs={{0,0},{1,32},{32,1},{33,33},{2,2},{3,34},{34,3},{35,35},{4,4},{5,3... | collective-permute-start | bytes 12296 | tf_op jit(solution)/shard_map/ppermute | solution.py:292
  67.0 0.6 copy-start.5
  67.0 1.6 %copy-start = (bf16[128,2,16,384]{3,2,1,0:T(8,128)(2,1)}, bf16[128,2,16,384]{3,2,1,0:T(8,128)(2,1)S(1)}, u32[]{:S(2)}) copy-start(bf16[128,2,16,384]{3,2,1,0:T(8,128)(2,1)S(1)} %all-to-all-done) | copy-start | bytes 9437188
  75.7 47.4 %copy-start.4 = (bf16[128,2,2,128]{3,0,1,2:T(8,128)(2,1)S(1)}, bf16[128,2,2,128]{3,0,1,2:T(8,128)(2,1)}, u32[]{:S(2)}) copy-start(bf16[128,2,2,128]{3,0,1,2:T(8,128)(2,1)} %constant.32.clone) | copy-start | bytes 393220
  75.7 16.5 %collective-permute-start.3 = (bf16[256,2048]{1,0:T(8,128)(2,1)}, bf16[256,2048]{1,0:T(8,128)(2,1)S(1)}, u32[]{:S(2)}, u32[]{:S(2)}) collective-permute-start(bf16[256,2048]{1,0:T(8,128)(2,1)} %weights.1.own), channel_id=1, source_target_pairs={{32,0},{2,32},{34,2},{4,34},{36,4},{6,36},{38,6},{8,38},{40,8},{10... | collective-permute-start | bytes 3145736 | tf_op jit(solution)/shard_map/ppermute | solution.py:298
  77.8 15.7 %collective-permute-start.2 = (bf16[256,2048]{1,0:T(8,128)(2,1)}, bf16[256,2048]{1,0:T(8,128)(2,1)S(1)}, u32[]{:S(2)}, u32[]{:S(2)}) collective-permute-start(bf16[256,2048]{1,0:T(8,128)(2,1)} %weights.1.own), channel_id=1, source_target_pairs={{0,32},{32,2},{2,34},{34,4},{4,36},{36,6},{6,38},{38,8},{8,40},{40... | collective-permute-start | bytes 3145736 | tf_op jit(solution)/shard_map/ppermute | solution.py:297
  92.2 1.3 %copy-start.1 = (bf16[256,2048]{1,0:T(8,128)(2,1)}, bf16[256,2048]{1,0:T(8,128)(2,1)S(1)}, u32[]{:S(2)}) copy-start(bf16[256,2048]{1,0:T(8,128)(2,1)S(1)} %collective-permute-done.3.higher) | copy-start | bytes 3145732
  93.5 1.0 copy-start.2

commit v2 on v1

v2 whole, which is shorter than its diff:
```python
import functools
import math

import jax
import jax.numpy as jnp
import ml_dtypes
import numpy as np
from jax import lax
from jax.experimental import pallas as pl
from jax.experimental.pallas import tpu as pltpu
from jax.sharding import Mesh
from jax.sharding import PartitionSpec as P

FREQUENCY_BINS = 128
LOAD_PCT = 10
KEEP_PCT = 50
PHASE_STEPS = 4096

PARTS = ("zh", "core", "x", "y", "zl")
SIZES = (2, 2, 4, 4, 2)
SOLVER = ("zh", "zl", "x", "y", "core")
DEVICES = 128

ANTENNAS = 2048
BEAMS = 128
SPECTRA = 384
HERE = 16
TAIL = 16
PIECES = 2
PIECE = ANTENNAS // PIECES
CHUNK = 512
COLUMNS = 256

BLOCK = 16384

BF = jnp.bfloat16
F32 = jnp.float32
ANY = pl.BlockSpec(memory_space=pl.ANY)
VMEM = pl.BlockSpec(memory_space=pltpu.VMEM)
SMEM = pl.BlockSpec(memory_space=pltpu.SMEM)


TURNED = (((1,), (1,)), ((), ()))


def solver_index():
    grid = np.arange(DEVICES).reshape(SIZES)
    return np.transpose(grid, (0, 4, 2, 3, 1)).reshape(-1)


def fourier_matrix(length, sign):
    counter = np.arange(length, dtype=np.int64)
    angle = (counter[:, None] * counter[None, :] % length) * (2.0 * math.pi / length)
    cosine = np.cos(angle) / math.sqrt(length)
    sine = sign * np.sin(angle) / math.sqrt(length)
    table = np.stack([np.stack([cosine, sine], axis=1), np.stack([-sine, cosine], axis=1)], axis=0)
    return table.astype(np.float32).astype(ml_dtypes.bfloat16)


def dot(a, b):
    return jnp.dot(a, b, preferred_element_type=F32)


def placed(space, *operands):
    return [pltpu.with_memory_space_constraint(x, space) for x in operands]


def channelize_kernel(table, voltages, out, rows, turned):
    step = BLOCK // FREQUENCY_BINS
    for p in range(2):
        for s in range(step):
            tile = voltages[p, :, s * FREQUENCY_BINS : (s + 1) * FREQUENCY_BINS]
            rows[p, s * HERE : (s + 1) * HERE] = tile.astype(F32)
    for a in range(HERE):
        mine = pl.ds(a, step, stride=HERE)
        signal = jnp.concatenate([rows[0, mine], rows[1, mine]], axis=1).astype(BF)
        spectrum = lax.dot_general(table[...], signal, TURNED, preferred_element_type=F32)
        turned[pl.ds(a, 2 * FREQUENCY_BINS, stride=HERE)] = spectrum
    out[...] = turned[...].astype(BF).reshape(FREQUENCY_BINS, 2, HERE, step)


def channelize(voltages):
    step = BLOCK // FREQUENCY_BINS
    table = fourier_matrix(FREQUENCY_BINS, -1.0)[..., solver_index()]
    table = table.transpose(3, 2, 0, 1).reshape(2 * FREQUENCY_BINS, 2 * FREQUENCY_BINS)
    return pl.pallas_call(
        channelize_kernel,
        grid=(SPECTRA // step,),
        in_specs=[
            pl.BlockSpec(table.shape, lambda j: (0, 0)),
            pl.BlockSpec((2, HERE, BLOCK), lambda j: (0, 0, j)),
        ],
        out_specs=pl.BlockSpec((FREQUENCY_BINS, 2, HERE, step), lambda j: (0, 0, 0, j)),
        out_shape=pltpu.HBM((FREQUENCY_BINS, 2, HERE, SPECTRA), BF),
        scratch_shapes=[
            pltpu.VMEM((2, step * HERE, FREQUENCY_BINS), F32),
            pltpu.VMEM((2 * FREQUENCY_BINS * HERE, step), F32),
        ],
        compiler_params=pltpu.CompilerParams(vmem_limit_bytes=40 << 20),
        name="channelize",
    )(*placed(pltpu.HBM, jnp.asarray(table), voltages))


def steering(pos, directions, channel):
    phase = ((pos * directions) & (PHASE_STEPS - 1)) * (channel + FREQUENCY_BINS)
    moved = (phase & (PHASE_STEPS - 1)) + 512
    quadrant = moved >> 10
    x = ((moved & 1023) - 512).astype(F32) * (2.0 * math.pi / PHASE_STEPS)
    y = x * x
    sine = 1.0 / 362880.0
    for c in (-1.0 / 5040.0, 1.0 / 120.0, -1.0 / 6.0, 1.0):
        sine = sine * y + c
    sine = sine * x
    cosine = 1.0 / 40320.0
    for c in (-1.0 / 720.0, 1.0 / 24.0, -0.5, 1.0):
        cosine = cosine * y + c
    odd = (quadrant & 1) == 1
    c = jnp.where(odd, sine, cosine)
    s = jnp.where(odd, cosine, sine)
    c = jnp.where(((quadrant + 1) & 2) == 2, -c, c)
    s = jnp.where((quadrant & 2) == 2, -s, s)
    return c, s


def earlier_kernel(channels, pos, directions, trace, earlier, *rest):
    product, (steer, coarse, own) = rest[:PIECES], rest[PIECES:]
    j = pl.program_id(0)

    @pl.when(j == 0)
    def _():
        for i in range(ANTENNAS // COLUMNS):
            at = slice(i * COLUMNS, (i + 1) * COLUMNS)
            c, s = steering(pos[:, at], directions[...], channels[0])
            own[:BEAMS, at] = c.astype(BF)
            own[BEAMS:, at] = s.astype(BF)

    here = pl.ds(pl.multiple_of(j * COLUMNS, COLUMNS), COLUMNS)
    c, s = steering(pos[:, here], directions[...], channels[1])
    steer[:BEAMS] = c
    steer[BEAMS:] = s
    coarse[:BEAMS] = c.astype(BF)
    coarse[BEAMS:] = s.astype(BF)
    first = dot(own[...], earlier[0, 0])
    second = dot(own[...], earlier[0, 1])
    total = jnp.sum(trace[...], keepdims=True)
    high = total.astype(BF)
    middle = (total - high.astype(F32)).astype(BF)
    low = (total - high.astype(F32) - middle.astype(F32)).astype(BF)
    row = lax.broadcasted_iota(jnp.int32, (TAIL, COLUMNS), 0)
    tail = jnp.where(row == 2, low.astype(F32), 0.0)
    tail = jnp.where(row == 1, middle.astype(F32), tail)
    tail = jnp.where(row == 0, high.astype(F32), tail).astype(BF)
    for i in range(PIECES):

        @pl.when(j // (PIECE // COLUMNS) == i)
        def _():
            product[i][:BEAMS] = (first[:BEAMS] + second[BEAMS:]).astype(BF)
            product[i][BEAMS : 2 * BEAMS] = (first[BEAMS:] - second[:BEAMS]).astype(BF)
            product[i][2 * BEAMS :] = tail


def diagonal_kernel(earlier, trace):
    @pl.when(pl.program_id(0) == 0)
    def _():
        trace[...] = jnp.zeros_like(trace)

    square = earlier[0, 0].astype(F32)
    row = lax.broadcasted_iota(jnp.int32, square.shape, 0)
    column = lax.broadcasted_iota(jnp.int32, square.shape, 1)
    kept = jnp.where(row == column, square, 0.0)
    kept = jnp.sum(kept.reshape(COLUMNS // 8, 8, COLUMNS), axis=0)
    trace[...] += kept[:, :128] + kept[:, 128:]


def diagonal(earlier):
    return pl.pallas_call(
        diagonal_kernel,
        grid=(ANTENNAS // COLUMNS,),
        in_specs=[pl.BlockSpec((1, 1, COLUMNS, COLUMNS), lambda j: (0, 0, j, j))],
        out_specs=pl.BlockSpec((8, 128), lambda j: (0, 0)),
        out_shape=jax.ShapeDtypeStruct((8, 128), F32),
        compiler_params=pltpu.CompilerParams(vmem_limit_bytes=8 << 20),
        name="diagonal",
    )(*placed(pltpu.HBM, earlier))


def piece_block(i):
    steps = PIECE // COLUMNS
    return pl.BlockSpec((2 * BEAMS + TAIL, COLUMNS), lambda j: (0, jnp.clip(j - i * steps, 0, steps - 1)))


def earlier_product(channels, pos, directions, trace, earlier):
    steps = ANTENNAS // COLUMNS
    wide = pl.BlockSpec((2 * BEAMS, COLUMNS), lambda j: (0, j))
    return pl.pallas_call(
        earlier_kernel,
        grid=(steps,),
        in_specs=[
            SMEM,
            pl.BlockSpec((1, ANTENNAS), lambda j: (0, 0)),
            pl.BlockSpec((BEAMS, 1), lambda j: (0, 0)),
            pl.BlockSpec((8, 128), lambda j: (0, 0)),
            pl.BlockSpec((1, 2, ANTENNAS, COLUMNS), lambda j: (0, 0, 0, j)),
        ],
        out_specs=[piece_block(i) for i in range(PIECES)] + [wide, wide],
        out_shape=[pltpu.HBM((2 * BEAMS + TAIL, PIECE), BF)] * PIECES
        + [
            pltpu.HBM((2 * BEAMS, ANTENNAS), F32),
            pltpu.HBM((2 * BEAMS, ANTENNAS), BF),
        ],
        scratch_shapes=[pltpu.VMEM((2 * BEAMS, ANTENNAS), BF)],
        compiler_params=pltpu.CompilerParams(vmem_limit_bytes=20 << 20),
        name="earlier_product",
    )(channels, pos, directions, trace, *placed(pltpu.HBM, earlier))


def antennas_of(here, part, chunk):
    at = pl.ds(chunk * (CHUNK // HERE), CHUNK // HERE)
    return here[at, part].reshape(CHUNK, SPECTRA)


def data_kernel(here, coarse_hbm, steer_hbm, *rest):
    data, steer, power, (coarse, sems) = rest[:PIECES], rest[PIECES : 2 * PIECES], rest[2 * PIECES], rest[2 * PIECES + 1 :]
    copies = [pltpu.make_async_copy(coarse_hbm, coarse, sems.at[0])]
    for i in range(PIECES):
        source = steer_hbm.at[:, pl.ds(i * PIECE, PIECE)]
        copies.append(pltpu.make_async_copy(source, steer[i], sems.at[1 + i]))
    for c in copies:
        c.start()
    total = jnp.zeros((8, SPECTRA), F32)
    for chunk in range(ANTENNAS // CHUNK):
        for part in range(2):
            x = antennas_of(here, part, chunk).astype(F32).reshape(CHUNK // 8, 8, SPECTRA)
            total += jnp.sum(x * x, axis=0)
    power[...] = total
    copies[0].wait()
    first = jnp.zeros((2 * BEAMS, SPECTRA), F32)
    second = jnp.zeros((2 * BEAMS, SPECTRA), F32)
    for chunk in range(ANTENNAS // CHUNK):
        at = slice(chunk * CHUNK, (chunk + 1) * CHUNK)
        first += dot(coarse[:, at], antennas_of(here, 0, chunk))
        second += dot(coarse[:, at], antennas_of(here, 1, chunk))
    inner = jnp.concatenate(
        [first[:BEAMS] + second[BEAMS:], first[BEAMS:] - second[:BEAMS]], axis=0
    ).astype(BF)
    for chunk in range(ANTENNAS // CHUNK):
        piece, offset = divmod(chunk * CHUNK, PIECE)
        at = slice(offset, offset + CHUNK)
        p = lax.dot_general(inner, antennas_of(here, 0, chunk), TURNED, preferred_element_type=F32)
        q = lax.dot_general(inner, antennas_of(here, 1, chunk), TURNED, preferred_element_type=F32)
        data[piece][:BEAMS, at] = p[:BEAMS] - q[BEAMS:]
        data[piece][BEAMS:, at] = p[BEAMS:] + q[:BEAMS]
    for c in copies[1:]:
        c.wait()


def data_product(here, coarse, steer):
    piece = pltpu.VMEM((2 * BEAMS, PIECE), F32)
    out = pl.pallas_call(
        data_kernel,
        in_specs=[VMEM, ANY, ANY],
        out_specs=[VMEM] * (2 * PIECES + 1),
        out_shape=[piece] * (2 * PIECES) + [pltpu.VMEM((8, SPECTRA), F32)],
        scratch_shapes=[pltpu.VMEM((2 * BEAMS, ANTENNAS), BF), pltpu.SemaphoreType.DMA((1 + PIECES,))],
        compiler_params=pltpu.CompilerParams(vmem_limit_bytes=12 << 20),
        name="data_product",
    )(*placed(pltpu.VMEM, here), *placed(pltpu.HBM, coarse, steer))
    return out[:PIECES], out[PIECES : 2 * PIECES], out[2 * PIECES]


def weights_kernel(data, steer, power, trace, product, out):
    keep = KEEP_PCT / 100.0
    fresh = (1.0 - keep) / SPECTRA
    total = jnp.sum(power[...], keepdims=True) * fresh + jnp.sum(trace[2 * BEAMS :, :1].astype(F32), keepdims=True) * keep
    mean_diag = total * (1.0 / ANTENNAS)
    loading = LOAD_PCT / 100.0 * mean_diag
    upper = 5.0 * mean_diag
    center = 0.5 * (upper + loading)
    radius = 0.5 * (upper - loading)
    ratio = center / radius
    factor = 1.0 / ratio
    factor_next = 1.0 / (2.0 * ratio - factor)
    beta = 2.0 * factor_next / (radius * center)
    alpha = (1.0 + factor_next * factor) / center + 2.0 * factor_next / radius
    out[...] = (
        (alpha - beta * loading) * steer[...]
        - (keep * beta) * product[: 2 * BEAMS].astype(F32)
        - (fresh * beta) * data[...]
    ).astype(BF)


def weigh(*operands):
    return pl.pallas_call(
        weights_kernel,
        in_specs=[VMEM] * 5,
        out_specs=VMEM,
        out_shape=pltpu.VMEM((2 * BEAMS, PIECE), BF),
        compiler_params=pltpu.CompilerParams(vmem_limit_bytes=8 << 20),
        name="weights",
    )(*placed(pltpu.VMEM, *operands))


def beams_kernel(piece, here, own, chip, link, *rest):
    *before, out = rest
    if before:
        first, second = before[0][0], before[0][1]
    else:
        first = jnp.zeros((2 * BEAMS, SPECTRA), F32)
        second = jnp.zeros((2 * BEAMS, SPECTRA), F32)
    for chunk in range(PIECE // CHUNK):
        at = slice(chunk * CHUNK, (chunk + 1) * CHUNK)
        smooth = (
            0.25 * (chip[:, at].astype(F32) + link[:, at].astype(F32)) + 0.5 * own[:, at].astype(F32)
        ).astype(BF)
        first += dot(smooth, antennas_of(here, 0, piece * (PIECE // CHUNK) + chunk))
        second += dot(smooth, antennas_of(here, 1, piece * (PIECE // CHUNK) + chunk))
    if piece < PIECES - 1:
        out[0] = first
        out[1] = second
    else:
        out[0] = (first[:BEAMS] + second[BEAMS:]).astype(BF)
        out[1] = (second[:BEAMS] - first[BEAMS:]).astype(BF)


def form_beams(piece, *operands):
    last = piece == PIECES - 1
    out = pltpu.VMEM((2, BEAMS, SPECTRA), BF) if last else pltpu.VMEM((2, 2 * BEAMS, SPECTRA), F32)
    return pl.pallas_call(
        functools.partial(beams_kernel, piece),
        in_specs=[VMEM] * len(operands),
        out_specs=VMEM,
        out_shape=out,
        compiler_params=pltpu.CompilerParams(vmem_limit_bytes=12 << 20),
        name="form_beams",
    )(*placed(pltpu.VMEM, *operands))


def shards(voltages, earlier, antenna_pos, beam_dir):
    spectra = channelize(voltages)
    here = lax.all_to_all(spectra, PARTS, split_axis=0, concat_axis=0, tiled=True)

    channels = jnp.stack([lax.axis_index(PARTS), lax.axis_index(SOLVER)]).astype(jnp.int32)
    *product, steer, coarse = earlier_product(
        channels,
        antenna_pos.reshape(1, ANTENNAS),
        beam_dir.reshape(BEAMS, 1),
        diagonal(earlier),
        earlier,
    )
    swap = [(0, 0), (1, 2), (2, 1), (3, 3)]
    product = [lax.ppermute(x, ("core", "zl"), swap) for x in product]
    trace = product[0]

    data, steer, power = data_product(here, coarse, steer)

    holder = np.argsort(solver_index()).tolist()
    pairs = list(zip(holder[1:-1:2], holder[2::2]))
    pairs = pairs + [(b, a) for a, b in pairs]
    sides = []
    for i in range(PIECES):
        weights = weigh(data[i], steer[i], power, trace, product[i])
        link = lax.ppermute(weights, PARTS, pairs)
        chip = lax.ppermute(weights, "core", [(0, 1), (1, 0)])
        sides.append((weights, chip, link))
    sums = ()
    for i in range(PIECES):
        sums = (form_beams(i, here, *sides[i], *sums),)
    beamed = sums[0]
    turned = lax.all_to_all(beamed.transpose(1, 0, 2), PARTS, split_axis=0, concat_axis=0, tiled=True)
    inverse = fourier_matrix(FREQUENCY_BINS, 1.0).transpose(1, 0, 2, 3)[solver_index()]
    series = jnp.einsum("kps,kpqt->qst", turned, inverse, preferred_element_type=F32)
    return series.reshape(1, 2, SPECTRA * FREQUENCY_BINS)


def solution(mesh):
    fine = Mesh(mesh.devices.reshape(SIZES), PARTS)
    placed = (P(None, PARTS, None), P(PARTS, None, None, None), P(), P())
    return jax.shard_map(
        shards, mesh=fine, in_specs=placed, out_specs=P(PARTS, None, None), check_vma=False
    )
```

time: 125 us -> 106 us (0.85)
  waiting for transfers between devices: 39.6 us -> 25.5 us
  local copies, waits for them, and re-layouts: 11.9 us -> 1.55 us
  Pallas kernels: 25.3 us -> 33.6 us
  blocking collectives: 22.8 us -> 21.3 us
    ppermute x4 -> x6, waiting for transfers between devices: 39.6 us -> 7.78 us  [the longest x2 7.77 us: shards(): link = lax.ppermute(weights, PARTS, pairs)]
    all_to_all x1, waiting for transfers between devices: 0.01 us -> 17.7 us  [shards(): lax.all_to_all(spectra, PARTS, split_axis=0, concat_axis=0, tiled=True)]
    pallas_call x2 -> x7, Pallas kernels: 11.6 us -> 19.7 us  [the longest x1 7.06 us: channelize(): pl.pallas_call(channelize_kernel, grid=(SPECTRA // step,), in_specs=[pl.B...]
    unnamed x15 -> x6, local copies, waits for them, and re-layouts: 5.3 us -> 0.02 us
    convert_element_type x1 -> x0, local copies, waits for them, and re-layouts: 3.49 us -> none  [shards(): spectra = jnp.einsum('ptqk,past->kqas', fourier_matrix(FREQUENCY_BINS, -1...]
    all_to_all x1, blocking collectives: 22.8 us -> 21.3 us  [shards(): lax.all_to_all(beamed.transpose(1, 0, 2), PARTS, split_axis=0, concat_axi...]
    ppermute x4 -> x6, starting transfers between devices: 11.3 us -> 11.3 us  [the longest x2 5.57 us: shards(): product = [lax.ppermute(x, ('core', 'zl'), swap) for x in product]]
  transfers between devices with their start and end apart: 5 -> 7, of which waited for: 3 -> 3; matrix products, arithmetic and copies ran while one was open for 1% -> 0% of each run, Pallas kernels for 11% -> 25%
where the time goes in v2:
time: 106 us; the launch traced here: 105 us
  Pallas kernels  33.6 us (32%)
  waiting for transfers between devices  25.5 us (24%)
  starting transfers between devices  22.8 us (22%)
  blocking collectives  21.3 us (20%)
  local copies, waits for them, and re-layouts  1.55 us (1%)
    all_to_all x1, blocking collectives, shards(): lax.all_to_all(beamed.transpose(1, 0, 2), PARTS, split_axis=0, concat_axi...  21.3 us
    all_to_all x1, waiting for transfers between devices, shards(): lax.all_to_all(spectra, PARTS, split_axis=0, concat_axis=0, tiled=True)  17.7 us
    pallas_call x1, Pallas kernels, earlier_product(): pl.pallas_call(earlier_kernel, grid=(steps,), in_specs=[SMEM, pl.BlockSpe...  13.9 us
    all_to_all x1, starting transfers between devices, shards(): lax.all_to_all(spectra, PARTS, split_axis=0, concat_axis=0, tiled=True)  11.5 us
    ppermute x2, waiting for transfers between devices, shards(): link = lax.ppermute(weights, PARTS, pairs)  7.77 us
    pallas_call x1, Pallas kernels, channelize(): pl.pallas_call(channelize_kernel, grid=(SPECTRA // step,), in_specs=[pl.B...  7.06 us
    ppermute x2, starting transfers between devices, shards(): product = [lax.ppermute(x, ('core', 'zl'), swap) for x in product]  5.57 us
    ppermute x2, starting transfers between devices, shards(): link = lax.ppermute(weights, PARTS, pairs)  5.56 us
  transfers between devices with their start and end apart: 7, of which 3 were waited for; matrix products, arithmetic and copies ran while one was open for 0% of the time, Pallas kernels for 25%

profile of v2, /device:TPU:1, one launch (start us, length us, event | category | flops | bytes accessed | tf_op | source)
XLA Modules:
  0.0 105.2 jit_solution(5499526646975647068)
XLA Ops:
  0.0 7.1 %channelize.1 = bf16[128,2,16,384]{3,2,1,0:T(8,128)(2,1)} custom-call(bf16[256,256]{1,0:T(8,128)(2,1)} %constant.31.clone.table, bf16[2,16,49152]{2,1,0:T(8,128)(2,1)} %voltages.1), custom_call_target="tpu_custom_call" | custom-call | tf_op jit(solution)/shard_map/channelize/pallas_call | solution.py:86
  7.1 11.5 %all-to-all-start = ((bf16[128,2,16,384]{3,2,1,0:T(8,128)(2,1)}), bf16[128,2,16,384]{3,2,1,0:T(8,128)(2,1)S(1)}, u32[]{:S(2)}, u32[]{:S(2)}) async-start(bf16[128,2,16,384]{3,2,1,0:T(8,128)(2,1)} %channelize.1), calls=%async_computation | async-start | bytes 6291456 | tf_op jit(solution)/shard_map/all_to_all | solution.py:340
  18.6 0.0 copy-start.2
  18.6 0.0 copy-start
  18.6 3.9 %diagonal.1.trace = f32[8,128]{1,0:T(8,128)S(1)} custom-call(bf16[1,2,2048,2048]{3,2,1,0:T(8,128)(2,1)} %earlier.3), custom_call_target="tpu_custom_call" | custom-call | tf_op jit(solution)/shard_map/diagonal/pallas_call | solution.py:176
  22.5 0.0 copy-done.2
  22.5 0.1 copy.9.directions
  22.6 0.1 pad_add_fusion.channels
  22.7 0.0 copy-done
  22.7 13.9 %earlier_product.1 = (bf16[272,1024]{1,0:T(8,128)(2,1)}, bf16[272,1024]{1,0:T(8,128)(2,1)}, f32[256,2048]{1,0:T(8,128)}, bf16[256,2048]{1,0:T(8,128)(2,1)}) custom-call(s32[2]{0:T(128)S(1)} %pad_add_fusion.channels, s32[1,2048]{1,0:T(1,128)S(1)} %bitcast.15, s32[128,1]{1,0:T(8,128)S(1)} %copy.9.directions, f32[8,128]{1,0:T(8,128)S(1)} %diagonal.1.trace, ...), custom_call_target="tpu_custom_call" | custom-call | tf_op jit(solution)/shard_map/earlier_product/pallas_call | solution.py:195
  36.6 3.7 %collective-permute-start = (bf16[272,1024]{1,0:T(8,128)(2,1)}, bf16[272,1024]{1,0:T(8,128)(2,1)}, u32[]{:S(2)}, u32[]{:S(2)}) collective-permute-start(bf16[272,1024]{1,0:T(8,128)(2,1)} %get-tuple-element.19), channel_id=1, source_target_pairs={{0,0},{1,32},{32,1},{33,33},{2,2},{3,34},{34,3},{35,35},{4,4},{5,3... | collective-permute-start | bytes 1671176 | tf_op jit(solution)/shard_map/ppermute | solution.py:351
  40.2 1.9 %collective-permute-start.1 = (bf16[272,1024]{1,0:T(8,128)(2,1)}, bf16[272,1024]{1,0:T(8,128)(2,1)}, u32[]{:S(2)}, u32[]{:S(2)}) collective-permute-start(bf16[272,1024]{1,0:T(8,128)(2,1)} %get-tuple-element.20), channel_id=1, source_target_pairs={{0,0},{1,32},{32,1},{33,33},{2,2},{3,34},{34,3},{35,35},{4,4},{5,3... | collective-permute-start | bytes 1671176 | tf_op jit(solution)/shard_map/ppermute | solution.py:351
  42.2 17.7 %all-to-all-done.here = bf16[128,2,16,384]{3,2,1,0:T(8,128)(2,1)S(1)} async-done(((bf16[128,2,16,384]{3,2,1,0:T(8,128)(2,1)}), bf16[128,2,16,384]{3,2,1,0:T(8,128)(2,1)S(1)}, u32[]{:S(2)}, u32[]{:S(2)}) %all-to-all-start) | async-done | bytes 3145760 | tf_op jit(solution)/shard_map/all_to_all | solution.py:340
  59.9 3.7 %data_product.1 = (f32[256,1024]{1,0:T(8,128)S(1)}, f32[256,1024]{1,0:T(8,128)S(1)}, f32[256,1024]{1,0:T(8,128)S(1)}, f32[256,1024]{1,0:T(8,128)S(1)}, f32[8,384]{1,0:T(8,128)S(1)}) custom-call(bf16[128,2,16,384]{3,2,1,0:T(8,128)(2,1)S(1)} %all-to-all-done.here, bf16[256,2048]{1,0:T(8,128)(2,1)} %get-tuple-element.14.coarse_hbm, ...), custom_call_target="tpu_custom_call" | custom-call | tf_op jit(solution)/shard_map/data_product/pallas_call | solution.py:259
  63.6 0.0 collective-permute-done.trace.product
  63.6 1.8 %weights.3.own = bf16[256,1024]{1,0:T(8,128)(2,1)S(1)} custom-call(f32[256,1024]{1,0:T(8,128)S(1)} %get-tuple-element.21.data, f32[256,1024]{1,0:T(8,128)S(1)} %get-tuple-element.22.steer, f32[8,384]{1,0:T(8,128)S(1)} %get-tuple-element.18.power, bf16[272,1024]{1,0:T(8,128)(2,1)} %collective-permute-done.trace.product, ...), custom_call_target="tpu_custom_call" | custom-call | tf_op jit(solution)/shard_map/weights/pallas_call | solution.py:293
  65.4 2.9 %collective-permute-start.5 = (bf16[256,1024]{1,0:T(8,128)(2,1)S(1)}, bf16[256,1024]{1,0:T(8,128)(2,1)S(1)}, u32[]{:S(2)}, u32[]{:S(2)}) collective-permute-start(bf16[256,1024]{1,0:T(8,128)(2,1)S(1)} %weights.3.own), channel_id=1, source_target_pairs={{32,2},{34,4},{36,6},{38,8},{40,10},{42,12},{44,14},{46,16},{48,18... | collective-permute-start | bytes 1572872 | tf_op jit(solution)/shard_map/ppermute | solution.py:362
  68.4 0.1 collective-permute-start.4
  68.5 0.0 collective-permute-done.1.product
  68.5 1.8 %weights.2.own = bf16[256,1024]{1,0:T(8,128)(2,1)S(1)} custom-call(f32[256,1024]{1,0:T(8,128)S(1)} %get-tuple-element.16.data, f32[256,1024]{1,0:T(8,128)S(1)} %get-tuple-element.17.steer, f32[8,384]{1,0:T(8,128)S(1)} %get-tuple-element.18.power, bf16[272,1024]{1,0:T(8,128)(2,1)} %collective-permute-done.trace.product, ...), custom_call_target="tpu_custom_call" | custom-call | tf_op jit(solution)/shard_map/weights/pallas_call | solution.py:293
  70.3 2.7 %collective-permute-start.3 = (bf16[256,1024]{1,0:T(8,128)(2,1)S(1)}, bf16[256,1024]{1,0:T(8,128)(2,1)S(1)}, u32[]{:S(2)}, u32[]{:S(2)}) collective-permute-start(bf16[256,1024]{1,0:T(8,128)(2,1)S(1)} %weights.2.own), channel_id=1, source_target_pairs={{32,2},{34,4},{36,6},{38,8},{40,10},{42,12},{44,14},{46,16},{48,18... | collective-permute-start | bytes 1572872 | tf_op jit(solution)/shard_map/ppermute | solution.py:362
  73.0 0.1 collective-permute-start.2
  73.1 2.9 %collective-permute-done.5.link = bf16[256,1024]{1,0:T(8,128)(2,1)S(1)} collective-permute-done((bf16[256,1024]{1,0:T(8,128)(2,1)S(1)}, bf16[256,1024]{1,0:T(8,128)(2,1)S(1)}, u32[]{:S(2)}, u32[]{:S(2)}) %collective-permute-start.5) | collective-permute-done | bytes 524320 | tf_op jit(solution)/shard_map/ppermute | solution.py:362
  75.9 0.0 collective-permute-done.4.chip
  75.9 0.7 form_beams.2.rest_0_
  76.7 0.0 copy-start.1
  76.7 4.9 %collective-permute-done.3.link = bf16[256,1024]{1,0:T(8,128)(2,1)S(1)} collective-permute-done((bf16[256,1024]{1,0:T(8,128)(2,1)S(1)}, bf16[256,1024]{1,0:T(8,128)(2,1)S(1)}, u32[]{:S(2)}, u32[]{:S(2)}) %collective-permute-start.3) | collective-permute-done | bytes 524320 | tf_op jit(solution)/shard_map/ppermute | solution.py:362
  81.6 0.0 collective-permute-done.2.chip
  81.6 0.7 form_beams.3
  82.3 0.2 copy.10
  82.5 21.3 %all_to_all.10 = bf16[128,2,384]{2,1,0:T(2,128)(2,1)S(1)} all-to-all(bf16[128,2,384]{2,1,0:T(2,128)(2,1)S(1)} %copy.10), channel_id=1, replica_groups=mesh['zh'=2,'core'=2,'x'=4,'y'=4,'zl'=2] {'zh','core','x','y','zl'}, dimensions={0} | all-to-all | bytes 393216 | tf_op jit(solution)/shard_map/all_to_all | solution.py:369
  103.8 0.2 copy.11
  104.0 0.0 copy-done.1
  104.0 0.2 convolution_bitcast_fusion
  104.2 1.0 reshape.11
Async XLA Ops:
  7.1 52.8 %all-to-all-start = ((bf16[128,2,16,384]{3,2,1,0:T(8,128)(2,1)}), bf16[128,2,16,384]{3,2,1,0:T(8,128)(2,1)S(1)}, u32[]{:S(2)}, u32[]{:S(2)}) async-start(bf16[128,2,16,384]{3,2,1,0:T(8,128)(2,1)} %channelize.1), calls=%async_computation | async-start | bytes 6291456 | tf_op jit(solution)/shard_map/all_to_all | solution.py:340
  18.6 3.9 %copy-start.2 = (s32[128]{0:T(128)S(1)}, s32[128]{0:T(128)}, u32[]{:S(2)}) copy-start(s32[128]{0:T(128)} %param.9) | copy-start | bytes 1540
  18.6 4.1 %copy-start = (s32[2048]{0:T(1024)S(1)}, s32[2048]{0:T(1024)}, u32[]{:S(2)}) copy-start(s32[2048]{0:T(1024)} %param.8) | copy-start | bytes 24580
  36.6 27.0 %collective-permute-start = (bf16[272,1024]{1,0:T(8,128)(2,1)}, bf16[272,1024]{1,0:T(8,128)(2,1)}, u32[]{:S(2)}, u32[]{:S(2)}) collective-permute-start(bf16[272,1024]{1,0:T(8,128)(2,1)} %get-tuple-element.19), channel_id=1, source_target_pairs={{0,0},{1,32},{32,1},{33,33},{2,2},{3,34},{34,3},{35,35},{4,4},{5,3... | collective-permute-start | bytes 1671176 | tf_op jit(solution)/shard_map/ppermute | solution.py:351
  40.2 28.2 %collective-permute-start.1 = (bf16[272,1024]{1,0:T(8,128)(2,1)}, bf16[272,1024]{1,0:T(8,128)(2,1)}, u32[]{:S(2)}, u32[]{:S(2)}) collective-permute-start(bf16[272,1024]{1,0:T(8,128)(2,1)} %get-tuple-element.20), channel_id=1, source_target_pairs={{0,0},{1,32},{32,1},{33,33},{2,2},{3,34},{34,3},{35,35},{4,4},{5,3... | collective-permute-start | bytes 1671176 | tf_op jit(solution)/shard_map/ppermute | solution.py:351
  65.4 10.5 %collective-permute-start.5 = (bf16[256,1024]{1,0:T(8,128)(2,1)S(1)}, bf16[256,1024]{1,0:T(8,128)(2,1)S(1)}, u32[]{:S(2)}, u32[]{:S(2)}) collective-permute-start(bf16[256,1024]{1,0:T(8,128)(2,1)S(1)} %weights.3.own), channel_id=1, source_target_pairs={{32,2},{34,4},{36,6},{38,8},{40,10},{42,12},{44,14},{46,16},{48,18... | collective-permute-start | bytes 1572872 | tf_op jit(solution)/shard_map/ppermute | solution.py:362
  68.4 7.6 %collective-permute-start.4 = (bf16[256,1024]{1,0:T(8,128)(2,1)S(1)}, bf16[256,1024]{1,0:T(8,128)(2,1)S(1)}, u32[]{:S(2)}, u32[]{:S(2)}) collective-permute-start(bf16[256,1024]{1,0:T(8,128)(2,1)S(1)} %weights.3.own), channel_id=1, source_target_pairs={{0,32},{32,0},{1,33},{33,1},{2,34},{34,2},{3,35},{35,3},{4,36},{36... | collective-permute-start | bytes 1572872 | tf_op jit(solution)/shard_map/ppermute | solution.py:363
  70.3 11.3 %collective-permute-start.3 = (bf16[256,1024]{1,0:T(8,128)(2,1)S(1)}, bf16[256,1024]{1,0:T(8,128)(2,1)S(1)}, u32[]{:S(2)}, u32[]{:S(2)}) collective-permute-start(bf16[256,1024]{1,0:T(8,128)(2,1)S(1)} %weights.2.own), channel_id=1, source_target_pairs={{32,2},{34,4},{36,6},{38,8},{40,10},{42,12},{44,14},{46,16},{48,18... | collective-permute-start | bytes 1572872 | tf_op jit(solution)/shard_map/ppermute | solution.py:362
  73.0 8.6 %collective-permute-start.2 = (bf16[256,1024]{1,0:T(8,128)(2,1)S(1)}, bf16[256,1024]{1,0:T(8,128)(2,1)S(1)}, u32[]{:S(2)}, u32[]{:S(2)}) collective-permute-start(bf16[256,1024]{1,0:T(8,128)(2,1)S(1)} %weights.2.own), channel_id=1, source_target_pairs={{0,32},{32,0},{1,33},{33,1},{2,34},{34,2},{3,35},{35,3},{4,36},{36... | collective-permute-start | bytes 1572872 | tf_op jit(solution)/shard_map/ppermute | solution.py:363
  76.7 27.3 %copy-start.1 = (bf16[128,2,2,128]{3,0,1,2:T(8,128)(2,1)S(1)}, bf16[128,2,2,128]{3,0,1,2:T(8,128)(2,1)}, u32[]{:S(2)}) copy-start(bf16[128,2,2,128]{3,0,1,2:T(8,128)(2,1)} %constant.32.clone) | copy-start | bytes 393220

commit v3 on v2

--- a/solution.py
+++ b/solution.py
@@ -31,7 +31,7 @@
 CHUNK = 512
 COLUMNS = 256
 
-BLOCK = 16384
+GROUP = 8
 
 BF = jnp.bfloat16
 F32 = jnp.float32
@@ -66,35 +66,36 @@
 
 
 def channelize_kernel(table, voltages, out, rows, turned):
-    step = BLOCK // FREQUENCY_BINS
     for p in range(2):
-        for s in range(step):
+        for s in range(SPECTRA):
             tile = voltages[p, :, s * FREQUENCY_BINS : (s + 1) * FREQUENCY_BINS]
-            rows[p, s * HERE : (s + 1) * HERE] = tile.astype(F32)
-    for a in range(HERE):
-        mine = pl.ds(a, step, stride=HERE)
+            rows[p, s * GROUP : (s + 1) * GROUP] = tile.astype(F32)
+    for a in range(GROUP):
+        mine = pl.ds(a, SPECTRA, stride=GROUP)
         signal = jnp.concatenate([rows[0, mine], rows[1, mine]], axis=1).astype(BF)
         spectrum = lax.dot_general(table[...], signal, TURNED, preferred_element_type=F32)
-        turned[pl.ds(a, 2 * FREQUENCY_BINS, stride=HERE)] = spectrum
-    out[...] = turned[...].astype(BF).reshape(FREQUENCY_BINS, 2, HERE, step)
+        for b in range(SPECTRA // 128):
+            turned[b, pl.ds(a, 2 * FREQUENCY_BINS, stride=GROUP)] = spectrum[:, b * 128 : (b + 1) * 128]
+    for b in range(SPECTRA // 128):
+        block = turned[b].astype(BF).reshape(FREQUENCY_BINS, 2, GROUP, 128)
+        out[:, :, :, b * 128 : (b + 1) * 128] = block
 
 
 def channelize(voltages):
-    step = BLOCK // FREQUENCY_BINS
     table = fourier_matrix(FREQUENCY_BINS, -1.0)[..., solver_index()]
     table = table.transpose(3, 2, 0, 1).reshape(2 * FREQUENCY_BINS, 2 * FREQUENCY_BINS)
     return pl.pallas_call(
         channelize_kernel,
-        grid=(SPECTRA // step,),
+        grid=(HERE // GROUP,),
         in_specs=[
-            pl.BlockSpec(table.shape, lambda j: (0, 0)),
-            pl.BlockSpec((2, HERE, BLOCK), lambda j: (0, 0, j)),
+            pl.BlockSpec(table.shape, lambda i: (0, 0)),
+            pl.BlockSpec((2, GROUP, SPECTRA * FREQUENCY_BINS), lambda i: (0, i, 0)),
         ],
-        out_specs=pl.BlockSpec((FREQUENCY_BINS, 2, HERE, step), lambda j: (0, 0, 0, j)),
+        out_specs=pl.BlockSpec((FREQUENCY_BINS, 2, GROUP, SPECTRA), lambda i: (0, 0, i, 0)),
         out_shape=pltpu.HBM((FREQUENCY_BINS, 2, HERE, SPECTRA), BF),
         scratch_shapes=[
-            pltpu.VMEM((2, step * HERE, FREQUENCY_BINS), F32),
-            pltpu.VMEM((2 * FREQUENCY_BINS * HERE, step), F32),
+            pltpu.VMEM((2, SPECTRA * GROUP, FREQUENCY_BINS), F32),
+            pltpu.VMEM((SPECTRA // 128, 2 * FREQUENCY_BINS * GROUP, 128), F32),
         ],
         compiler_params=pltpu.CompilerParams(vmem_limit_bytes=40 << 20),
         name="channelize",
@@ -335,6 +336,23 @@
     )(*placed(pltpu.VMEM, *operands))
 
 
+def series_kernel(beams, inverse, out):
+    series = lax.dot_general(beams[...], inverse[...], (((0,), (0,)), ((), ())), preferred_element_type=F32)
+    for q in range(2):
+        out[pl.ds(q, SPECTRA, stride=2)] = series[:, q * FREQUENCY_BINS : (q + 1) * FREQUENCY_BINS]
+
+
+def resynthesize(beams, inverse):
+    return pl.pallas_call(
+        series_kernel,
+        in_specs=[VMEM, VMEM],
+        out_specs=VMEM,
+        out_shape=jax.ShapeDtypeStruct((2 * SPECTRA, FREQUENCY_BINS), F32),
+        compiler_params=pltpu.CompilerParams(vmem_limit_bytes=12 << 20),
+        name="resynthesize",
+    )(*placed(pltpu.VMEM, beams, inverse))
+
+
 def shards(voltages, earlier, antenna_pos, beam_dir):
     spectra = channelize(voltages)
     here = lax.all_to_all(spectra, PARTS, split_axis=0, concat_axis=0, tiled=True)
@@ -368,8 +386,8 @@
     beamed = sums[0]
     turned = lax.all_to_all(beamed.transpose(1, 0, 2), PARTS, split_axis=0, concat_axis=0, tiled=True)
     inverse = fourier_matrix(FREQUENCY_BINS, 1.0).transpose(1, 0, 2, 3)[solver_index()]
-    series = jnp.einsum("kps,kpqt->qst", turned, inverse, preferred_element_type=F32)
-    return series.reshape(1, 2, SPECTRA * FREQUENCY_BINS)
+    series = resynthesize(turned.reshape(2 * FREQUENCY_BINS, SPECTRA), jnp.asarray(inverse.reshape(2 * FREQUENCY_BINS, 2 * FREQUENCY_BINS)))
+    return series.reshape(SPECTRA, 2, FREQUENCY_BINS).transpose(1, 0, 2).reshape(1, 2, SPECTRA * FREQUENCY_BINS)
 
 
 def solution(mesh):

time: 106 us -> 105 us (level)
  local copies, waits for them, and re-layouts: 1.55 us -> 0.41 us
    pallas_call x1 -> x2, Pallas kernels: 7.06 us -> 6.65 us  [the longest x1 5.65 us: channelize(): pl.pallas_call(channelize_kernel, grid=(HERE // GROUP,), in_specs=[pl.Blo...]
where the time goes in v3:
time: 105 us; the launch traced here: 103 us
  Pallas kernels  33.2 us (32%)
  waiting for transfers between devices  25.5 us (24%)
  starting transfers between devices  22.8 us (22%)
  blocking collectives  21.3 us (20%)
    all_to_all x1, blocking collectives, shards(): lax.all_to_all(beamed.transpose(1, 0, 2), PARTS, split_axis=0, concat_axi...  21.3 us
    all_to_all x1, waiting for transfers between devices, shards(): lax.all_to_all(spectra, PARTS, split_axis=0, concat_axis=0, tiled=True)  17.7 us
    pallas_call x1, Pallas kernels, earlier_product(): pl.pallas_call(earlier_kernel, grid=(steps,), in_specs=[SMEM, pl.BlockSpe...  13.9 us
    all_to_all x1, starting transfers between devices, shards(): lax.all_to_all(spectra, PARTS, split_axis=0, concat_axis=0, tiled=True)  11.5 us
    ppermute x2, waiting for transfers between devices, shards(): link = lax.ppermute(weights, PARTS, pairs)  7.77 us
    pallas_call x1, Pallas kernels, channelize(): pl.pallas_call(channelize_kernel, grid=(HERE // GROUP,), in_specs=[pl.Blo...  5.65 us
    ppermute x2, starting transfers between devices, shards(): product = [lax.ppermute(x, ('core', 'zl'), swap) for x in product]  5.57 us
    ppermute x2, starting transfers between devices, shards(): link = lax.ppermute(weights, PARTS, pairs)  5.56 us
  transfers between devices with their start and end apart: 7, of which 3 were waited for; matrix products, arithmetic and copies ran while one was open for 0% of the time, Pallas kernels for 25%

profile of v3, /device:TPU:1, one launch (start us, length us, event | category | flops | bytes accessed | tf_op | source)
XLA Modules:
  0.0 103.5 jit_solution(17425568118415656049)
XLA Ops:
  0.0 5.6 %channelize.1 = bf16[128,2,16,384]{3,2,1,0:T(8,128)(2,1)} custom-call(bf16[256,256]{1,0:T(8,128)(2,1)} %constant.29.clone.table.inverse, bf16[2,16,49152]{2,1,0:T(8,128)(2,1)} %voltages.1), custom_call_target="tpu_custom_call" | custom-call | tf_op jit(solution)/shard_map/channelize/pallas_call | solution.py:87
  5.6 11.5 %all-to-all-start = ((bf16[128,2,16,384]{3,2,1,0:T(8,128)(2,1)}), bf16[128,2,16,384]{3,2,1,0:T(8,128)(2,1)S(1)}, u32[]{:S(2)}, u32[]{:S(2)}) async-start(bf16[128,2,16,384]{3,2,1,0:T(8,128)(2,1)} %channelize.1), calls=%async_computation | async-start | bytes 6291456 | tf_op jit(solution)/shard_map/all_to_all | solution.py:358
  17.2 0.0 copy-start.2
  17.2 0.0 copy-start.1
  17.2 3.9 %diagonal.1.trace = f32[8,128]{1,0:T(8,128)S(1)} custom-call(bf16[1,2,2048,2048]{3,2,1,0:T(8,128)(2,1)} %earlier.3), custom_call_target="tpu_custom_call" | custom-call | tf_op jit(solution)/shard_map/diagonal/pallas_call | solution.py:177
  21.1 0.0 copy-done.2
  21.1 0.1 copy.10.directions
  21.2 0.1 pad_add_fusion.channels
  21.3 0.0 copy-done.1
  21.3 13.9 %earlier_product.1 = (bf16[272,1024]{1,0:T(8,128)(2,1)}, bf16[272,1024]{1,0:T(8,128)(2,1)}, f32[256,2048]{1,0:T(8,128)}, bf16[256,2048]{1,0:T(8,128)(2,1)}) custom-call(s32[2]{0:T(128)S(1)} %pad_add_fusion.channels, s32[1,2048]{1,0:T(1,128)S(1)} %bitcast.11, s32[128,1]{1,0:T(8,128)S(1)} %copy.10.directions, f32[8,128]{1,0:T(8,128)S(1)} %diagonal.1.trace, ...), custom_call_target="tpu_custom_call" | custom-call | tf_op jit(solution)/shard_map/earlier_product/pallas_call | solution.py:196
  35.2 3.7 %collective-permute-start = (bf16[272,1024]{1,0:T(8,128)(2,1)}, bf16[272,1024]{1,0:T(8,128)(2,1)}, u32[]{:S(2)}, u32[]{:S(2)}) collective-permute-start(bf16[272,1024]{1,0:T(8,128)(2,1)} %get-tuple-element.19), channel_id=1, source_target_pairs={{0,0},{1,32},{32,1},{33,33},{2,2},{3,34},{34,3},{35,35},{4,4},{5,3... | collective-permute-start | bytes 1671176 | tf_op jit(solution)/shard_map/ppermute | solution.py:369
  38.8 1.9 %collective-permute-start.1 = (bf16[272,1024]{1,0:T(8,128)(2,1)}, bf16[272,1024]{1,0:T(8,128)(2,1)}, u32[]{:S(2)}, u32[]{:S(2)}) collective-permute-start(bf16[272,1024]{1,0:T(8,128)(2,1)} %get-tuple-element.20), channel_id=1, source_target_pairs={{0,0},{1,32},{32,1},{33,33},{2,2},{3,34},{34,3},{35,35},{4,4},{5,3... | collective-permute-start | bytes 1671176 | tf_op jit(solution)/shard_map/ppermute | solution.py:369
  40.8 17.7 %all-to-all-done.here = bf16[128,2,16,384]{3,2,1,0:T(8,128)(2,1)S(1)} async-done(((bf16[128,2,16,384]{3,2,1,0:T(8,128)(2,1)}), bf16[128,2,16,384]{3,2,1,0:T(8,128)(2,1)S(1)}, u32[]{:S(2)}, u32[]{:S(2)}) %all-to-all-start) | async-done | bytes 3145760 | tf_op jit(solution)/shard_map/all_to_all | solution.py:358
  58.5 3.7 %data_product.1 = (f32[256,1024]{1,0:T(8,128)S(1)}, f32[256,1024]{1,0:T(8,128)S(1)}, f32[256,1024]{1,0:T(8,128)S(1)}, f32[256,1024]{1,0:T(8,128)S(1)}, f32[8,384]{1,0:T(8,128)S(1)}) custom-call(bf16[128,2,16,384]{3,2,1,0:T(8,128)(2,1)S(1)} %all-to-all-done.here, bf16[256,2048]{1,0:T(8,128)(2,1)} %get-tuple-element.14.coarse_hbm, ...), custom_call_target="tpu_custom_call" | custom-call | tf_op jit(solution)/shard_map/data_product/pallas_call | solution.py:260
  62.2 0.0 collective-permute-done.trace.product
  62.2 1.8 %weights.3.own = bf16[256,1024]{1,0:T(8,128)(2,1)S(1)} custom-call(f32[256,1024]{1,0:T(8,128)S(1)} %get-tuple-element.21.data, f32[256,1024]{1,0:T(8,128)S(1)} %get-tuple-element.22.steer, f32[8,384]{1,0:T(8,128)S(1)} %get-tuple-element.18.power, bf16[272,1024]{1,0:T(8,128)(2,1)} %collective-permute-done.trace.product, ...), custom_call_target="tpu_custom_call" | custom-call | tf_op jit(solution)/shard_map/weights/pallas_call | solution.py:294
  64.0 2.9 %collective-permute-start.5 = (bf16[256,1024]{1,0:T(8,128)(2,1)S(1)}, bf16[256,1024]{1,0:T(8,128)(2,1)S(1)}, u32[]{:S(2)}, u32[]{:S(2)}) collective-permute-start(bf16[256,1024]{1,0:T(8,128)(2,1)S(1)} %weights.3.own), channel_id=1, source_target_pairs={{32,2},{34,4},{36,6},{38,8},{40,10},{42,12},{44,14},{46,16},{48,18... | collective-permute-start | bytes 1572872 | tf_op jit(solution)/shard_map/ppermute | solution.py:380
  67.0 0.1 collective-permute-start.4
  67.1 0.0 collective-permute-done.1.product
  67.1 1.8 %weights.2.own = bf16[256,1024]{1,0:T(8,128)(2,1)S(1)} custom-call(f32[256,1024]{1,0:T(8,128)S(1)} %get-tuple-element.16.data, f32[256,1024]{1,0:T(8,128)S(1)} %get-tuple-element.17.steer, f32[8,384]{1,0:T(8,128)S(1)} %get-tuple-element.18.power, bf16[272,1024]{1,0:T(8,128)(2,1)} %collective-permute-done.trace.product, ...), custom_call_target="tpu_custom_call" | custom-call | tf_op jit(solution)/shard_map/weights/pallas_call | solution.py:294
  68.9 2.7 %collective-permute-start.3 = (bf16[256,1024]{1,0:T(8,128)(2,1)S(1)}, bf16[256,1024]{1,0:T(8,128)(2,1)S(1)}, u32[]{:S(2)}, u32[]{:S(2)}) collective-permute-start(bf16[256,1024]{1,0:T(8,128)(2,1)S(1)} %weights.2.own), channel_id=1, source_target_pairs={{32,2},{34,4},{36,6},{38,8},{40,10},{42,12},{44,14},{46,16},{48,18... | collective-permute-start | bytes 1572872 | tf_op jit(solution)/shard_map/ppermute | solution.py:380
  71.6 0.1 collective-permute-start.2
  71.7 2.9 %collective-permute-done.5.link = bf16[256,1024]{1,0:T(8,128)(2,1)S(1)} collective-permute-done((bf16[256,1024]{1,0:T(8,128)(2,1)S(1)}, bf16[256,1024]{1,0:T(8,128)(2,1)S(1)}, u32[]{:S(2)}, u32[]{:S(2)}) %collective-permute-start.5) | collective-permute-done | bytes 524320 | tf_op jit(solution)/shard_map/ppermute | solution.py:380
  74.5 0.0 collective-permute-done.4.chip
  74.5 0.7 form_beams.2.rest_0_
  75.3 0.0 copy-start
  75.3 4.9 %collective-permute-done.3.link = bf16[256,1024]{1,0:T(8,128)(2,1)S(1)} collective-permute-done((bf16[256,1024]{1,0:T(8,128)(2,1)S(1)}, bf16[256,1024]{1,0:T(8,128)(2,1)S(1)}, u32[]{:S(2)}, u32[]{:S(2)}) %collective-permute-start.3) | collective-permute-done | bytes 524320 | tf_op jit(solution)/shard_map/ppermute | solution.py:380
  80.2 0.0 collective-permute-done.2.chip
  80.2 0.7 form_beams.3
  80.9 0.2 copy.11
  81.1 21.3 %all_to_all.10 = bf16[128,2,384]{2,1,0:T(2,128)(2,1)S(1)} all-to-all(bf16[128,2,384]{2,1,0:T(2,128)(2,1)S(1)} %copy.11), channel_id=1, replica_groups=mesh['zh'=2,'core'=2,'x'=4,'y'=4,'zl'=2] {'zh','core','x','y','zl'}, dimensions={0} | all-to-all | bytes 393216 | tf_op jit(solution)/shard_map/all_to_all | solution.py:387
  102.4 0.1 reshape.17.beams
  102.5 0.0 copy-done
  102.5 1.0 resynthesize.1
Async XLA Ops:
  5.6 52.8 %all-to-all-start = ((bf16[128,2,16,384]{3,2,1,0:T(8,128)(2,1)}), bf16[128,2,16,384]{3,2,1,0:T(8,128)(2,1)S(1)}, u32[]{:S(2)}, u32[]{:S(2)}) async-start(bf16[128,2,16,384]{3,2,1,0:T(8,128)(2,1)} %channelize.1), calls=%async_computation | async-start | bytes 6291456 | tf_op jit(solution)/shard_map/all_to_all | solution.py:358
  17.2 3.9 %copy-start.2 = (s32[128]{0:T(128)S(1)}, s32[128]{0:T(128)}, u32[]{:S(2)}) copy-start(s32[128]{0:T(128)} %param.9) | copy-start | bytes 1540
  17.2 4.1 %copy-start.1 = (s32[2048]{0:T(1024)S(1)}, s32[2048]{0:T(1024)}, u32[]{:S(2)}) copy-start(s32[2048]{0:T(1024)} %param.8) | copy-start | bytes 24580
  35.2 27.0 %collective-permute-start = (bf16[272,1024]{1,0:T(8,128)(2,1)}, bf16[272,1024]{1,0:T(8,128)(2,1)}, u32[]{:S(2)}, u32[]{:S(2)}) collective-permute-start(bf16[272,1024]{1,0:T(8,128)(2,1)} %get-tuple-element.19), channel_id=1, source_target_pairs={{0,0},{1,32},{32,1},{33,33},{2,2},{3,34},{34,3},{35,35},{4,4},{5,3... | collective-permute-start | bytes 1671176 | tf_op jit(solution)/shard_map/ppermute | solution.py:369
  38.8 28.2 %collective-permute-start.1 = (bf16[272,1024]{1,0:T(8,128)(2,1)}, bf16[272,1024]{1,0:T(8,128)(2,1)}, u32[]{:S(2)}, u32[]{:S(2)}) collective-permute-start(bf16[272,1024]{1,0:T(8,128)(2,1)} %get-tuple-element.20), channel_id=1, source_target_pairs={{0,0},{1,32},{32,1},{33,33},{2,2},{3,34},{34,3},{35,35},{4,4},{5,3... | collective-permute-start | bytes 1671176 | tf_op jit(solution)/shard_map/ppermute | solution.py:369
  64.0 10.5 %collective-permute-start.5 = (bf16[256,1024]{1,0:T(8,128)(2,1)S(1)}, bf16[256,1024]{1,0:T(8,128)(2,1)S(1)}, u32[]{:S(2)}, u32[]{:S(2)}) collective-permute-start(bf16[256,1024]{1,0:T(8,128)(2,1)S(1)} %weights.3.own), channel_id=1, source_target_pairs={{32,2},{34,4},{36,6},{38,8},{40,10},{42,12},{44,14},{46,16},{48,18... | collective-permute-start | bytes 1572872 | tf_op jit(solution)/shard_map/ppermute | solution.py:380
  67.0 7.6 %collective-permute-start.4 = (bf16[256,1024]{1,0:T(8,128)(2,1)S(1)}, bf16[256,1024]{1,0:T(8,128)(2,1)S(1)}, u32[]{:S(2)}, u32[]{:S(2)}) collective-permute-start(bf16[256,1024]{1,0:T(8,128)(2,1)S(1)} %weights.3.own), channel_id=1, source_target_pairs={{0,32},{32,0},{1,33},{33,1},{2,34},{34,2},{3,35},{35,3},{4,36},{36... | collective-permute-start | bytes 1572872 | tf_op jit(solution)/shard_map/ppermute | solution.py:381
  68.9 11.3 %collective-permute-start.3 = (bf16[256,1024]{1,0:T(8,128)(2,1)S(1)}, bf16[256,1024]{1,0:T(8,128)(2,1)S(1)}, u32[]{:S(2)}, u32[]{:S(2)}) collective-permute-start(bf16[256,1024]{1,0:T(8,128)(2,1)S(1)} %weights.2.own), channel_id=1, source_target_pairs={{32,2},{34,4},{36,6},{38,8},{40,10},{42,12},{44,14},{46,16},{48,18... | collective-permute-start | bytes 1572872 | tf_op jit(solution)/shard_map/ppermute | solution.py:380
  71.6 8.6 %collective-permute-start.2 = (bf16[256,1024]{1,0:T(8,128)(2,1)S(1)}, bf16[256,1024]{1,0:T(8,128)(2,1)S(1)}, u32[]{:S(2)}, u32[]{:S(2)}) collective-permute-start(bf16[256,1024]{1,0:T(8,128)(2,1)S(1)} %weights.2.own), channel_id=1, source_target_pairs={{0,32},{32,0},{1,33},{33,1},{2,34},{34,2},{3,35},{35,3},{4,36},{36... | collective-permute-start | bytes 1572872 | tf_op jit(solution)/shard_map/ppermute | solution.py:381
  75.3 27.2 %copy-start = (bf16[256,256]{1,0:T(8,128)(2,1)S(1)}, bf16[256,256]{1,0:T(8,128)(2,1)}, u32[]{:S(2)}) copy-start(bf16[256,256]{1,0:T(8,128)(2,1)} %constant.29.clone.table.inverse) | copy-start | bytes 393220

commit v4 on v3

--- a/solution.py
+++ b/solution.py
@@ -269,10 +269,17 @@
     return out[:PIECES], out[PIECES : 2 * PIECES], out[2 * PIECES]
 
 
-def weights_kernel(data, steer, power, trace, product, out):
+def weights_kernel(data, steer, power, trace_hbm, product_hbm, out, trace, product, sems):
+    copies = [
+        pltpu.make_async_copy(trace_hbm.at[pl.ds(2 * BEAMS, TAIL), pl.ds(0, 128)], trace, sems.at[0]),
+        pltpu.make_async_copy(product_hbm.at[pl.ds(0, 2 * BEAMS)], product, sems.at[1]),
+    ]
+    for c in copies:
+        c.start()
+    copies[0].wait()
     keep = KEEP_PCT / 100.0
     fresh = (1.0 - keep) / SPECTRA
-    total = jnp.sum(power[...], keepdims=True) * fresh + jnp.sum(trace[2 * BEAMS :, :1].astype(F32), keepdims=True) * keep
+    total = jnp.sum(power[...], keepdims=True) * fresh + jnp.sum(trace[:, :1].astype(F32), keepdims=True) * keep
     mean_diag = total * (1.0 / ANTENNAS)
     loading = LOAD_PCT / 100.0 * mean_diag
     upper = 5.0 * mean_diag
@@ -283,22 +290,28 @@
     factor_next = 1.0 / (2.0 * ratio - factor)
     beta = 2.0 * factor_next / (radius * center)
     alpha = (1.0 + factor_next * factor) / center + 2.0 * factor_next / radius
+    copies[1].wait()
     out[...] = (
         (alpha - beta * loading) * steer[...]
-        - (keep * beta) * product[: 2 * BEAMS].astype(F32)
+        - (keep * beta) * product[...].astype(F32)
         - (fresh * beta) * data[...]
     ).astype(BF)
 
 
-def weigh(*operands):
+def weigh(data, steer, power, trace, product):
     return pl.pallas_call(
         weights_kernel,
-        in_specs=[VMEM] * 5,
+        in_specs=[VMEM, VMEM, VMEM, ANY, ANY],
         out_specs=VMEM,
         out_shape=pltpu.VMEM((2 * BEAMS, PIECE), BF),
+        scratch_shapes=[
+            pltpu.VMEM((TAIL, 128), BF),
+            pltpu.VMEM((2 * BEAMS, PIECE), BF),
+            pltpu.SemaphoreType.DMA((2,)),
+        ],
         compiler_params=pltpu.CompilerParams(vmem_limit_bytes=8 << 20),
         name="weights",
-    )(*placed(pltpu.VMEM, *operands))
+    )(*placed(pltpu.VMEM, data, steer, power), *placed(pltpu.HBM, trace, product))
 
 
 def beams_kernel(piece, here, own, chip, link, *rest):

time: 105 us -> 104 us (level)
    pallas_call x2, Pallas kernels: 3.66 us -> 2.59 us  [weigh(): pl.pallas_call(weights_kernel, in_specs=[VMEM, VMEM, VMEM, ANY, ANY], out...]
  transfers between devices with their start and end apart: 7 -> 7, of which waited for: 3 -> 4; matrix products, arithmetic and copies ran while one was open for 0% -> 0% of each run, Pallas kernels for 25% -> 24%
where the time goes in v4:
time: 104 us; the launch traced here: 102 us
  Pallas kernels  32.2 us (31%)
  waiting for transfers between devices  26.1 us (25%)
  starting transfers between devices  22.8 us (22%)
  blocking collectives  20.7 us (20%)
    all_to_all x1, blocking collectives, shards(): lax.all_to_all(beamed.transpose(1, 0, 2), PARTS, split_axis=0, concat_axi...  20.7 us
    all_to_all x1, waiting for transfers between devices, shards(): lax.all_to_all(spectra, PARTS, split_axis=0, concat_axis=0, tiled=True)  17.7 us
    pallas_call x1, Pallas kernels, earlier_product(): pl.pallas_call(earlier_kernel, grid=(steps,), in_specs=[SMEM, pl.BlockSpe...  13.9 us
    all_to_all x1, starting transfers between devices, shards(): lax.all_to_all(spectra, PARTS, split_axis=0, concat_axis=0, tiled=True)  11.5 us
    ppermute x2, waiting for transfers between devices, shards(): link = lax.ppermute(weights, PARTS, pairs)  8.3 us
    pallas_call x1, Pallas kernels, channelize(): pl.pallas_call(channelize_kernel, grid=(HERE // GROUP,), in_specs=[pl.Blo...  5.65 us
    ppermute x2, starting transfers between devices, shards(): product = [lax.ppermute(x, ('core', 'zl'), swap) for x in product]  5.57 us
    ppermute x2, starting transfers between devices, shards(): link = lax.ppermute(weights, PARTS, pairs)  5.52 us
  transfers between devices with their start and end apart: 7, of which 4 were waited for; matrix products, arithmetic and copies ran while one was open for 0% of the time, Pallas kernels for 24%

profile of v4, /device:TPU:1, one launch (start us, length us, event | category | flops | bytes accessed | tf_op | source)
XLA Modules:
  0.0 102.4 jit_solution(4344478979916013836)
XLA Ops:
  0.0 5.6 %channelize.1 = bf16[128,2,16,384]{3,2,1,0:T(8,128)(2,1)} custom-call(bf16[256,256]{1,0:T(8,128)(2,1)} %constant.29.clone.table.inverse, bf16[2,16,49152]{2,1,0:T(8,128)(2,1)} %voltages.1), custom_call_target="tpu_custom_call" | custom-call | tf_op jit(solution)/shard_map/channelize/pallas_call | solution.py:87
  5.6 11.5 %all-to-all-start = ((bf16[128,2,16,384]{3,2,1,0:T(8,128)(2,1)}), bf16[128,2,16,384]{3,2,1,0:T(8,128)(2,1)S(1)}, u32[]{:S(2)}, u32[]{:S(2)}) async-start(bf16[128,2,16,384]{3,2,1,0:T(8,128)(2,1)} %channelize.1), calls=%async_computation | async-start | bytes 6291456 | tf_op jit(solution)/shard_map/all_to_all | solution.py:371
  17.2 0.0 copy-start.2
  17.2 0.0 copy-start.1
  17.2 3.9 %diagonal.1.trace = f32[8,128]{1,0:T(8,128)S(1)} custom-call(bf16[1,2,2048,2048]{3,2,1,0:T(8,128)(2,1)} %earlier.3), custom_call_target="tpu_custom_call" | custom-call | tf_op jit(solution)/shard_map/diagonal/pallas_call | solution.py:177
  21.1 0.0 copy-done.2
  21.1 0.1 copy.10.directions
  21.2 0.1 pad_add_fusion.channels
  21.3 0.0 copy-done.1
  21.3 13.9 %earlier_product.1 = (bf16[272,1024]{1,0:T(8,128)(2,1)}, bf16[272,1024]{1,0:T(8,128)(2,1)}, f32[256,2048]{1,0:T(8,128)}, bf16[256,2048]{1,0:T(8,128)(2,1)}) custom-call(s32[2]{0:T(128)S(1)} %pad_add_fusion.channels, s32[1,2048]{1,0:T(1,128)S(1)} %bitcast.11, s32[128,1]{1,0:T(8,128)S(1)} %copy.10.directions, f32[8,128]{1,0:T(8,128)S(1)} %diagonal.1.trace, ...), custom_call_target="tpu_custom_call" | custom-call | tf_op jit(solution)/shard_map/earlier_product/pallas_call | solution.py:196
  35.2 3.7 %collective-permute-start = (bf16[272,1024]{1,0:T(8,128)(2,1)}, bf16[272,1024]{1,0:T(8,128)(2,1)}, u32[]{:S(2)}, u32[]{:S(2)}) collective-permute-start(bf16[272,1024]{1,0:T(8,128)(2,1)} %get-tuple-element.19), channel_id=1, source_target_pairs={{0,0},{1,32},{32,1},{33,33},{2,2},{3,34},{34,3},{35,35},{4,4},{5,3... | collective-permute-start | bytes 1671176 | tf_op jit(solution)/shard_map/ppermute | solution.py:382
  38.8 1.9 %collective-permute-start.1 = (bf16[272,1024]{1,0:T(8,128)(2,1)}, bf16[272,1024]{1,0:T(8,128)(2,1)}, u32[]{:S(2)}, u32[]{:S(2)}) collective-permute-start(bf16[272,1024]{1,0:T(8,128)(2,1)} %get-tuple-element.20), channel_id=1, source_target_pairs={{0,0},{1,32},{32,1},{33,33},{2,2},{3,34},{34,3},{35,35},{4,4},{5,3... | collective-permute-start | bytes 1671176 | tf_op jit(solution)/shard_map/ppermute | solution.py:382
  40.8 17.7 %all-to-all-done.here = bf16[128,2,16,384]{3,2,1,0:T(8,128)(2,1)S(1)} async-done(((bf16[128,2,16,384]{3,2,1,0:T(8,128)(2,1)}), bf16[128,2,16,384]{3,2,1,0:T(8,128)(2,1)S(1)}, u32[]{:S(2)}, u32[]{:S(2)}) %all-to-all-start) | async-done | bytes 3145760 | tf_op jit(solution)/shard_map/all_to_all | solution.py:371
  58.5 3.7 %data_product.1 = (f32[256,1024]{1,0:T(8,128)S(1)}, f32[256,1024]{1,0:T(8,128)S(1)}, f32[256,1024]{1,0:T(8,128)S(1)}, f32[256,1024]{1,0:T(8,128)S(1)}, f32[8,384]{1,0:T(8,128)S(1)}) custom-call(bf16[128,2,16,384]{3,2,1,0:T(8,128)(2,1)S(1)} %all-to-all-done.here, bf16[256,2048]{1,0:T(8,128)(2,1)} %get-tuple-element.14.coarse_hbm, ...), custom_call_target="tpu_custom_call" | custom-call | tf_op jit(solution)/shard_map/data_product/pallas_call | solution.py:260
  62.2 0.0 collective-permute-done.trace_hbm.product_hbm
  62.2 1.3 %weights.3.own = bf16[256,1024]{1,0:T(8,128)(2,1)S(1)} custom-call(f32[256,1024]{1,0:T(8,128)S(1)} %get-tuple-element.21.data, f32[256,1024]{1,0:T(8,128)S(1)} %get-tuple-element.22.steer, f32[8,384]{1,0:T(8,128)S(1)} %get-tuple-element.18.power, bf16[272,1024]{1,0:T(8,128)(2,1)} %collective-permute-done.trace_hbm.product_hbm, ...), custom_call_target="tpu_custom_call" | custom-call | tf_op jit(solution)/shard_map/weights/pallas_call | solution.py:302
  63.5 2.9 %collective-permute-start.5 = (bf16[256,1024]{1,0:T(8,128)(2,1)S(1)}, bf16[256,1024]{1,0:T(8,128)(2,1)S(1)}, u32[]{:S(2)}, u32[]{:S(2)}) collective-permute-start(bf16[256,1024]{1,0:T(8,128)(2,1)S(1)} %weights.3.own), channel_id=1, source_target_pairs={{32,2},{34,4},{36,6},{38,8},{40,10},{42,12},{44,14},{46,16},{48,18... | collective-permute-start | bytes 1572872 | tf_op jit(solution)/shard_map/ppermute | solution.py:393
  66.4 0.1 collective-permute-start.4
  66.5 0.1 collective-permute-done.1.product_hbm
  66.6 1.3 %weights.2.own = bf16[256,1024]{1,0:T(8,128)(2,1)S(1)} custom-call(f32[256,1024]{1,0:T(8,128)S(1)} %get-tuple-element.16.data, f32[256,1024]{1,0:T(8,128)S(1)} %get-tuple-element.17.steer, f32[8,384]{1,0:T(8,128)S(1)} %get-tuple-element.18.power, bf16[272,1024]{1,0:T(8,128)(2,1)} %collective-permute-done.trace_hbm.product_hbm, ...), custom_call_target="tpu_custom_call" | custom-call | tf_op jit(solution)/shard_map/weights/pallas_call | solution.py:302
  67.9 2.6 %collective-permute-start.3 = (bf16[256,1024]{1,0:T(8,128)(2,1)S(1)}, bf16[256,1024]{1,0:T(8,128)(2,1)S(1)}, u32[]{:S(2)}, u32[]{:S(2)}) collective-permute-start(bf16[256,1024]{1,0:T(8,128)(2,1)S(1)} %weights.2.own), channel_id=1, source_target_pairs={{32,2},{34,4},{36,6},{38,8},{40,10},{42,12},{44,14},{46,16},{48,18... | collective-permute-start | bytes 1572872 | tf_op jit(solution)/shard_map/ppermute | solution.py:393
  70.5 0.1 collective-permute-start.2
  70.6 3.4 %collective-permute-done.5.link = bf16[256,1024]{1,0:T(8,128)(2,1)S(1)} collective-permute-done((bf16[256,1024]{1,0:T(8,128)(2,1)S(1)}, bf16[256,1024]{1,0:T(8,128)(2,1)S(1)}, u32[]{:S(2)}, u32[]{:S(2)}) %collective-permute-start.5) | collective-permute-done | bytes 524320 | tf_op jit(solution)/shard_map/ppermute | solution.py:393
  74.0 0.0 collective-permute-done.4.chip
  74.0 0.7 form_beams.2.rest_0_
  74.8 0.0 copy-start
  74.8 4.9 %collective-permute-done.3.link = bf16[256,1024]{1,0:T(8,128)(2,1)S(1)} collective-permute-done((bf16[256,1024]{1,0:T(8,128)(2,1)S(1)}, bf16[256,1024]{1,0:T(8,128)(2,1)S(1)}, u32[]{:S(2)}, u32[]{:S(2)}) %collective-permute-start.3) | collective-permute-done | bytes 524320 | tf_op jit(solution)/shard_map/ppermute | solution.py:393
  79.6 0.0 collective-permute-done.2.chip
  79.6 0.7 form_beams.3
  80.4 0.2 copy.11
  80.6 20.7 %all_to_all.10 = bf16[128,2,384]{2,1,0:T(2,128)(2,1)S(1)} all-to-all(bf16[128,2,384]{2,1,0:T(2,128)(2,1)S(1)} %copy.11), channel_id=1, replica_groups=mesh['zh'=2,'core'=2,'x'=4,'y'=4,'zl'=2] {'zh','core','x','y','zl'}, dimensions={0} | all-to-all | bytes 393216 | tf_op jit(solution)/shard_map/all_to_all | solution.py:400
  101.3 0.1 reshape.17.beams
  101.4 0.0 copy-done
  101.4 1.0 resynthesize.1
Async XLA Ops:
  5.6 52.8 %all-to-all-start = ((bf16[128,2,16,384]{3,2,1,0:T(8,128)(2,1)}), bf16[128,2,16,384]{3,2,1,0:T(8,128)(2,1)S(1)}, u32[]{:S(2)}, u32[]{:S(2)}) async-start(bf16[128,2,16,384]{3,2,1,0:T(8,128)(2,1)} %channelize.1), calls=%async_computation | async-start | bytes 6291456 | tf_op jit(solution)/shard_map/all_to_all | solution.py:371
  17.2 3.9 %copy-start.2 = (s32[128]{0:T(128)S(1)}, s32[128]{0:T(128)}, u32[]{:S(2)}) copy-start(s32[128]{0:T(128)} %param.9) | copy-start | bytes 1540
  17.2 4.1 %copy-start.1 = (s32[2048]{0:T(1024)S(1)}, s32[2048]{0:T(1024)}, u32[]{:S(2)}) copy-start(s32[2048]{0:T(1024)} %param.8) | copy-start | bytes 24580
  35.2 27.0 %collective-permute-start = (bf16[272,1024]{1,0:T(8,128)(2,1)}, bf16[272,1024]{1,0:T(8,128)(2,1)}, u32[]{:S(2)}, u32[]{:S(2)}) collective-permute-start(bf16[272,1024]{1,0:T(8,128)(2,1)} %get-tuple-element.19), channel_id=1, source_target_pairs={{0,0},{1,32},{32,1},{33,33},{2,2},{3,34},{34,3},{35,35},{4,4},{5,3... | collective-permute-start | bytes 1671176 | tf_op jit(solution)/shard_map/ppermute | solution.py:382
  38.8 27.8 %collective-permute-start.1 = (bf16[272,1024]{1,0:T(8,128)(2,1)}, bf16[272,1024]{1,0:T(8,128)(2,1)}, u32[]{:S(2)}, u32[]{:S(2)}) collective-permute-start(bf16[272,1024]{1,0:T(8,128)(2,1)} %get-tuple-element.20), channel_id=1, source_target_pairs={{0,0},{1,32},{32,1},{33,33},{2,2},{3,34},{34,3},{35,35},{4,4},{5,3... | collective-permute-start | bytes 1671176 | tf_op jit(solution)/shard_map/ppermute | solution.py:382
  63.5 10.5 %collective-permute-start.5 = (bf16[256,1024]{1,0:T(8,128)(2,1)S(1)}, bf16[256,1024]{1,0:T(8,128)(2,1)S(1)}, u32[]{:S(2)}, u32[]{:S(2)}) collective-permute-start(bf16[256,1024]{1,0:T(8,128)(2,1)S(1)} %weights.3.own), channel_id=1, source_target_pairs={{32,2},{34,4},{36,6},{38,8},{40,10},{42,12},{44,14},{46,16},{48,18... | collective-permute-start | bytes 1572872 | tf_op jit(solution)/shard_map/ppermute | solution.py:393
  66.4 7.6 %collective-permute-start.4 = (bf16[256,1024]{1,0:T(8,128)(2,1)S(1)}, bf16[256,1024]{1,0:T(8,128)(2,1)S(1)}, u32[]{:S(2)}, u32[]{:S(2)}) collective-permute-start(bf16[256,1024]{1,0:T(8,128)(2,1)S(1)} %weights.3.own), channel_id=1, source_target_pairs={{0,32},{32,0},{1,33},{33,1},{2,34},{34,2},{3,35},{35,3},{4,36},{36... | collective-permute-start | bytes 1572872 | tf_op jit(solution)/shard_map/ppermute | solution.py:394
  67.9 11.8 %collective-permute-start.3 = (bf16[256,1024]{1,0:T(8,128)(2,1)S(1)}, bf16[256,1024]{1,0:T(8,128)(2,1)S(1)}, u32[]{:S(2)}, u32[]{:S(2)}) collective-permute-start(bf16[256,1024]{1,0:T(8,128)(2,1)S(1)} %weights.2.own), channel_id=1, source_target_pairs={{32,2},{34,4},{36,6},{38,8},{40,10},{42,12},{44,14},{46,16},{48,18... | collective-permute-start | bytes 1572872 | tf_op jit(solution)/shard_map/ppermute | solution.py:393
  70.5 9.1 %collective-permute-start.2 = (bf16[256,1024]{1,0:T(8,128)(2,1)S(1)}, bf16[256,1024]{1,0:T(8,128)(2,1)S(1)}, u32[]{:S(2)}, u32[]{:S(2)}) collective-permute-start(bf16[256,1024]{1,0:T(8,128)(2,1)S(1)} %weights.2.own), channel_id=1, source_target_pairs={{0,32},{32,0},{1,33},{33,1},{2,34},{34,2},{3,35},{35,3},{4,36},{36... | collective-permute-start | bytes 1572872 | tf_op jit(solution)/shard_map/ppermute | solution.py:394
  74.8 26.6 %copy-start = (bf16[256,256]{1,0:T(8,128)(2,1)S(1)}, bf16[256,256]{1,0:T(8,128)(2,1)}, u32[]{:S(2)}) copy-start(bf16[256,256]{1,0:T(8,128)(2,1)} %constant.29.clone.table.inverse) | copy-start | bytes 393220

commit v5 on v4

--- a/solution.py
+++ b/solution.py
@@ -229,11 +229,14 @@
     for c in copies:
         c.start()
     total = jnp.zeros((8, SPECTRA), F32)
-    for chunk in range(ANTENNAS // CHUNK):
-        for part in range(2):
-            x = antennas_of(here, part, chunk).astype(F32).reshape(CHUNK // 8, 8, SPECTRA)
-            total += jnp.sum(x * x, axis=0)
-    power[...] = total
+
+    def squares(chunk):
+        parts = [antennas_of(here, part, chunk).astype(F32) for part in range(2)]
+        return sum(jnp.sum((x * x).reshape(CHUNK // 8, 8, SPECTRA), axis=0) for x in parts)
+
+    early = ANTENNAS // CHUNK // 2
+    for chunk in range(early):
+        total += squares(chunk)
     copies[0].wait()
     first = jnp.zeros((2 * BEAMS, SPECTRA), F32)
     second = jnp.zeros((2 * BEAMS, SPECTRA), F32)
@@ -241,6 +244,9 @@
         at = slice(chunk * CHUNK, (chunk + 1) * CHUNK)
         first += dot(coarse[:, at], antennas_of(here, 0, chunk))
         second += dot(coarse[:, at], antennas_of(here, 1, chunk))
+        if chunk >= early:
+            total += squares(chunk)
+    power[...] = total
     inner = jnp.concatenate(
         [first[:BEAMS] + second[BEAMS:], first[BEAMS:] - second[:BEAMS]], axis=0
     ).astype(BF)

time: 104 us -> 104 us (level)
  transfers between devices with their start and end apart: 7 -> 7, of which waited for: 4 -> 3; matrix products, arithmetic and copies ran while one was open for 0% -> 0% of each run, Pallas kernels for 24% -> 24%
where the time goes in v5:
time: 104 us; the launch traced here: 102 us
  Pallas kernels  32.2 us (31%)
  waiting for transfers between devices  26.1 us (25%)
  starting transfers between devices  22.8 us (22%)
  blocking collectives  20.8 us (20%)
    all_to_all x1, blocking collectives, shards(): lax.all_to_all(beamed.transpose(1, 0, 2), PARTS, split_axis=0, concat_axi...  20.8 us
    all_to_all x1, waiting for transfers between devices, shards(): lax.all_to_all(spectra, PARTS, split_axis=0, concat_axis=0, tiled=True)  17.7 us
    pallas_call x1, Pallas kernels, earlier_product(): pl.pallas_call(earlier_kernel, grid=(steps,), in_specs=[SMEM, pl.BlockSpe...  13.9 us
    all_to_all x1, starting transfers between devices, shards(): lax.all_to_all(spectra, PARTS, split_axis=0, concat_axis=0, tiled=True)  11.5 us
    ppermute x2, waiting for transfers between devices, shards(): link = lax.ppermute(weights, PARTS, pairs)  8.31 us
    pallas_call x1, Pallas kernels, channelize(): pl.pallas_call(channelize_kernel, grid=(HERE // GROUP,), in_specs=[pl.Blo...  5.65 us
    ppermute x2, starting transfers between devices, shards(): product = [lax.ppermute(x, ('core', 'zl'), swap) for x in product]  5.57 us
    ppermute x2, starting transfers between devices, shards(): link = lax.ppermute(weights, PARTS, pairs)  5.53 us
  transfers between devices with their start and end apart: 7, of which 3 were waited for; matrix products, arithmetic and copies ran while one was open for 0% of the time, Pallas kernels for 24%

profile of v5, /device:TPU:1, one launch (start us, length us, event | category | flops | bytes accessed | tf_op | source)
XLA Modules:
  0.0 102.4 jit_solution(15870212760935204490)
XLA Ops:
  0.0 5.6 %channelize.1 = bf16[128,2,16,384]{3,2,1,0:T(8,128)(2,1)} custom-call(bf16[256,256]{1,0:T(8,128)(2,1)} %constant.29.clone.table.inverse, bf16[2,16,49152]{2,1,0:T(8,128)(2,1)} %voltages.1), custom_call_target="tpu_custom_call" | custom-call | tf_op jit(solution)/shard_map/channelize/pallas_call | solution.py:87
  5.6 11.5 %all-to-all-start = ((bf16[128,2,16,384]{3,2,1,0:T(8,128)(2,1)}), bf16[128,2,16,384]{3,2,1,0:T(8,128)(2,1)S(1)}, u32[]{:S(2)}, u32[]{:S(2)}) async-start(bf16[128,2,16,384]{3,2,1,0:T(8,128)(2,1)} %channelize.1), calls=%async_computation | async-start | bytes 6291456 | tf_op jit(solution)/shard_map/all_to_all | solution.py:377
  17.2 0.0 copy-start.2
  17.2 0.0 copy-start.1
  17.2 3.9 %diagonal.1.trace = f32[8,128]{1,0:T(8,128)S(1)} custom-call(bf16[1,2,2048,2048]{3,2,1,0:T(8,128)(2,1)} %earlier.3), custom_call_target="tpu_custom_call" | custom-call | tf_op jit(solution)/shard_map/diagonal/pallas_call | solution.py:177
  21.1 0.0 copy-done.2
  21.1 0.1 copy.10.directions
  21.2 0.1 pad_add_fusion.channels
  21.3 0.0 copy-done.1
  21.3 13.9 %earlier_product.1 = (bf16[272,1024]{1,0:T(8,128)(2,1)}, bf16[272,1024]{1,0:T(8,128)(2,1)}, f32[256,2048]{1,0:T(8,128)}, bf16[256,2048]{1,0:T(8,128)(2,1)}) custom-call(s32[2]{0:T(128)S(1)} %pad_add_fusion.channels, s32[1,2048]{1,0:T(1,128)S(1)} %bitcast.11, s32[128,1]{1,0:T(8,128)S(1)} %copy.10.directions, f32[8,128]{1,0:T(8,128)S(1)} %diagonal.1.trace, ...), custom_call_target="tpu_custom_call" | custom-call | tf_op jit(solution)/shard_map/earlier_product/pallas_call | solution.py:196
  35.2 3.7 %collective-permute-start = (bf16[272,1024]{1,0:T(8,128)(2,1)}, bf16[272,1024]{1,0:T(8,128)(2,1)}, u32[]{:S(2)}, u32[]{:S(2)}) collective-permute-start(bf16[272,1024]{1,0:T(8,128)(2,1)} %get-tuple-element.19), channel_id=1, source_target_pairs={{0,0},{1,32},{32,1},{33,33},{2,2},{3,34},{34,3},{35,35},{4,4},{5,3... | collective-permute-start | bytes 1671176 | tf_op jit(solution)/shard_map/ppermute | solution.py:388
  38.8 1.9 %collective-permute-start.1 = (bf16[272,1024]{1,0:T(8,128)(2,1)}, bf16[272,1024]{1,0:T(8,128)(2,1)}, u32[]{:S(2)}, u32[]{:S(2)}) collective-permute-start(bf16[272,1024]{1,0:T(8,128)(2,1)} %get-tuple-element.20), channel_id=1, source_target_pairs={{0,0},{1,32},{32,1},{33,33},{2,2},{3,34},{34,3},{35,35},{4,4},{5,3... | collective-permute-start | bytes 1671176 | tf_op jit(solution)/shard_map/ppermute | solution.py:388
  40.8 17.7 %all-to-all-done.here = bf16[128,2,16,384]{3,2,1,0:T(8,128)(2,1)S(1)} async-done(((bf16[128,2,16,384]{3,2,1,0:T(8,128)(2,1)}), bf16[128,2,16,384]{3,2,1,0:T(8,128)(2,1)S(1)}, u32[]{:S(2)}, u32[]{:S(2)}) %all-to-all-start) | async-done | bytes 3145760 | tf_op jit(solution)/shard_map/all_to_all | solution.py:377
  58.5 3.7 %data_product.1 = (f32[256,1024]{1,0:T(8,128)S(1)}, f32[256,1024]{1,0:T(8,128)S(1)}, f32[256,1024]{1,0:T(8,128)S(1)}, f32[256,1024]{1,0:T(8,128)S(1)}, f32[8,384]{1,0:T(8,128)S(1)}) custom-call(bf16[128,2,16,384]{3,2,1,0:T(8,128)(2,1)S(1)} %all-to-all-done.here, bf16[256,2048]{1,0:T(8,128)(2,1)} %get-tuple-element.14.coarse_hbm, ...), custom_call_target="tpu_custom_call" | custom-call | tf_op jit(solution)/shard_map/data_product/pallas_call | solution.py:266
  62.2 0.0 collective-permute-done.trace_hbm.product_hbm
  62.2 1.3 %weights.3.own = bf16[256,1024]{1,0:T(8,128)(2,1)S(1)} custom-call(f32[256,1024]{1,0:T(8,128)S(1)} %get-tuple-element.21.data, f32[256,1024]{1,0:T(8,128)S(1)} %get-tuple-element.22.steer, f32[8,384]{1,0:T(8,128)S(1)} %get-tuple-element.18.power, bf16[272,1024]{1,0:T(8,128)(2,1)} %collective-permute-done.trace_hbm.product_hbm, ...), custom_call_target="tpu_custom_call" | custom-call | tf_op jit(solution)/shard_map/weights/pallas_call | solution.py:308
  63.5 2.9 %collective-permute-start.5 = (bf16[256,1024]{1,0:T(8,128)(2,1)S(1)}, bf16[256,1024]{1,0:T(8,128)(2,1)S(1)}, u32[]{:S(2)}, u32[]{:S(2)}) collective-permute-start(bf16[256,1024]{1,0:T(8,128)(2,1)S(1)} %weights.3.own), channel_id=1, source_target_pairs={{32,2},{34,4},{36,6},{38,8},{40,10},{42,12},{44,14},{46,16},{48,18... | collective-permute-start | bytes 1572872 | tf_op jit(solution)/shard_map/ppermute | solution.py:399
  66.4 0.1 collective-permute-start.4
  66.5 0.0 collective-permute-done.1.product_hbm
  66.6 1.3 %weights.2.own = bf16[256,1024]{1,0:T(8,128)(2,1)S(1)} custom-call(f32[256,1024]{1,0:T(8,128)S(1)} %get-tuple-element.16.data, f32[256,1024]{1,0:T(8,128)S(1)} %get-tuple-element.17.steer, f32[8,384]{1,0:T(8,128)S(1)} %get-tuple-element.18.power, bf16[272,1024]{1,0:T(8,128)(2,1)} %collective-permute-done.trace_hbm.product_hbm, ...), custom_call_target="tpu_custom_call" | custom-call | tf_op jit(solution)/shard_map/weights/pallas_call | solution.py:308
  67.9 2.6 %collective-permute-start.3 = (bf16[256,1024]{1,0:T(8,128)(2,1)S(1)}, bf16[256,1024]{1,0:T(8,128)(2,1)S(1)}, u32[]{:S(2)}, u32[]{:S(2)}) collective-permute-start(bf16[256,1024]{1,0:T(8,128)(2,1)S(1)} %weights.2.own), channel_id=1, source_target_pairs={{32,2},{34,4},{36,6},{38,8},{40,10},{42,12},{44,14},{46,16},{48,18... | collective-permute-start | bytes 1572872 | tf_op jit(solution)/shard_map/ppermute | solution.py:399
  70.5 0.1 collective-permute-start.2
  70.6 3.4 %collective-permute-done.5.link = bf16[256,1024]{1,0:T(8,128)(2,1)S(1)} collective-permute-done((bf16[256,1024]{1,0:T(8,128)(2,1)S(1)}, bf16[256,1024]{1,0:T(8,128)(2,1)S(1)}, u32[]{:S(2)}, u32[]{:S(2)}) %collective-permute-start.5) | collective-permute-done | bytes 524320 | tf_op jit(solution)/shard_map/ppermute | solution.py:399
  74.0 0.0 collective-permute-done.4.chip
  74.0 0.7 form_beams.2.rest_0_
  74.7 0.0 copy-start
  74.8 4.9 %collective-permute-done.3.link = bf16[256,1024]{1,0:T(8,128)(2,1)S(1)} collective-permute-done((bf16[256,1024]{1,0:T(8,128)(2,1)S(1)}, bf16[256,1024]{1,0:T(8,128)(2,1)S(1)}, u32[]{:S(2)}, u32[]{:S(2)}) %collective-permute-start.3) | collective-permute-done | bytes 524320 | tf_op jit(solution)/shard_map/ppermute | solution.py:399
  79.6 0.0 collective-permute-done.2.chip
  79.6 0.7 form_beams.3
  80.4 0.2 copy.11
  80.6 20.8 %all_to_all.10 = bf16[128,2,384]{2,1,0:T(2,128)(2,1)S(1)} all-to-all(bf16[128,2,384]{2,1,0:T(2,128)(2,1)S(1)} %copy.11), channel_id=1, replica_groups=mesh['zh'=2,'core'=2,'x'=4,'y'=4,'zl'=2] {'zh','core','x','y','zl'}, dimensions={0} | all-to-all | bytes 393216 | tf_op jit(solution)/shard_map/all_to_all | solution.py:406
  101.3 0.1 reshape.17.beams
  101.4 0.0 copy-done
  101.4 1.0 resynthesize.1
Async XLA Ops:
  5.6 52.8 %all-to-all-start = ((bf16[128,2,16,384]{3,2,1,0:T(8,128)(2,1)}), bf16[128,2,16,384]{3,2,1,0:T(8,128)(2,1)S(1)}, u32[]{:S(2)}, u32[]{:S(2)}) async-start(bf16[128,2,16,384]{3,2,1,0:T(8,128)(2,1)} %channelize.1), calls=%async_computation | async-start | bytes 6291456 | tf_op jit(solution)/shard_map/all_to_all | solution.py:377
  17.2 3.9 %copy-start.2 = (s32[128]{0:T(128)S(1)}, s32[128]{0:T(128)}, u32[]{:S(2)}) copy-start(s32[128]{0:T(128)} %param.9) | copy-start | bytes 1540
  17.2 4.1 %copy-start.1 = (s32[2048]{0:T(1024)S(1)}, s32[2048]{0:T(1024)}, u32[]{:S(2)}) copy-start(s32[2048]{0:T(1024)} %param.8) | copy-start | bytes 24580
  35.2 27.0 %collective-permute-start = (bf16[272,1024]{1,0:T(8,128)(2,1)}, bf16[272,1024]{1,0:T(8,128)(2,1)}, u32[]{:S(2)}, u32[]{:S(2)}) collective-permute-start(bf16[272,1024]{1,0:T(8,128)(2,1)} %get-tuple-element.19), channel_id=1, source_target_pairs={{0,0},{1,32},{32,1},{33,33},{2,2},{3,34},{34,3},{35,35},{4,4},{5,3... | collective-permute-start | bytes 1671176 | tf_op jit(solution)/shard_map/ppermute | solution.py:388
  38.8 27.8 %collective-permute-start.1 = (bf16[272,1024]{1,0:T(8,128)(2,1)}, bf16[272,1024]{1,0:T(8,128)(2,1)}, u32[]{:S(2)}, u32[]{:S(2)}) collective-permute-start(bf16[272,1024]{1,0:T(8,128)(2,1)} %get-tuple-element.20), channel_id=1, source_target_pairs={{0,0},{1,32},{32,1},{33,33},{2,2},{3,34},{34,3},{35,35},{4,4},{5,3... | collective-permute-start | bytes 1671176 | tf_op jit(solution)/shard_map/ppermute | solution.py:388
  63.5 10.5 %collective-permute-start.5 = (bf16[256,1024]{1,0:T(8,128)(2,1)S(1)}, bf16[256,1024]{1,0:T(8,128)(2,1)S(1)}, u32[]{:S(2)}, u32[]{:S(2)}) collective-permute-start(bf16[256,1024]{1,0:T(8,128)(2,1)S(1)} %weights.3.own), channel_id=1, source_target_pairs={{32,2},{34,4},{36,6},{38,8},{40,10},{42,12},{44,14},{46,16},{48,18... | collective-permute-start | bytes 1572872 | tf_op jit(solution)/shard_map/ppermute | solution.py:399
  66.4 7.6 %collective-permute-start.4 = (bf16[256,1024]{1,0:T(8,128)(2,1)S(1)}, bf16[256,1024]{1,0:T(8,128)(2,1)S(1)}, u32[]{:S(2)}, u32[]{:S(2)}) collective-permute-start(bf16[256,1024]{1,0:T(8,128)(2,1)S(1)} %weights.3.own), channel_id=1, source_target_pairs={{0,32},{32,0},{1,33},{33,1},{2,34},{34,2},{3,35},{35,3},{4,36},{36... | collective-permute-start | bytes 1572872 | tf_op jit(solution)/shard_map/ppermute | solution.py:400
  67.9 11.8 %collective-permute-start.3 = (bf16[256,1024]{1,0:T(8,128)(2,1)S(1)}, bf16[256,1024]{1,0:T(8,128)(2,1)S(1)}, u32[]{:S(2)}, u32[]{:S(2)}) collective-permute-start(bf16[256,1024]{1,0:T(8,128)(2,1)S(1)} %weights.2.own), channel_id=1, source_target_pairs={{32,2},{34,4},{36,6},{38,8},{40,10},{42,12},{44,14},{46,16},{48,18... | collective-permute-start | bytes 1572872 | tf_op jit(solution)/shard_map/ppermute | solution.py:399
  70.5 9.1 %collective-permute-start.2 = (bf16[256,1024]{1,0:T(8,128)(2,1)S(1)}, bf16[256,1024]{1,0:T(8,128)(2,1)S(1)}, u32[]{:S(2)}, u32[]{:S(2)}) collective-permute-start(bf16[256,1024]{1,0:T(8,128)(2,1)S(1)} %weights.2.own), channel_id=1, source_target_pairs={{0,32},{32,0},{1,33},{33,1},{2,34},{34,2},{3,35},{35,3},{4,36},{36... | collective-permute-start | bytes 1572872 | tf_op jit(solution)/shard_map/ppermute | solution.py:400
  74.7 26.7 %copy-start = (bf16[256,256]{1,0:T(8,128)(2,1)S(1)}, bf16[256,256]{1,0:T(8,128)(2,1)}, u32[]{:S(2)}) copy-start(bf16[256,256]{1,0:T(8,128)(2,1)} %constant.29.clone.table.inverse) | copy-start | bytes 393220
